TPU v7x, 512 devices: a whole 4x8x8 slice. The times are simulated.
512 devices in a mesh: seq: 64 (over y, z), tp: 8 (over x, core).
Axes of the slice: x: 4, y: 8, z: 8, core: 2. Of those that a mesh axis runs over, the one named last changes fastest.
Arguments:
- queries: bfloat16 [8, 8, 512, 8, 128], P(None, None, 'seq', 'tp'), may hold values from -16 to 16
- span_kv: bfloat16 [8, 8, 512, 256], P(None, None, 'seq'), may hold values from -12 to 12
- cache: bfloat16 [64, 2048, 256], P('seq', 'tp'), may hold values from -12 to 12, as said below
- prefix_len: int32 [8], replicated, may hold values from 1 to 2048, 8200 in all
- span_len: int32 [8], replicated, may hold values from 1 to 512, 2056 in all
- row_source: int32 [8, 512], replicated, may hold values from 0 to 511, each once within a row
Outputs:
- attended: bfloat16 [8, 8, 512, 8, 128], P(None, None, 'seq', 'tp')
Inputs may be any that keep to these rules, and one draw needn't show every extreme that they name: `cache`: cached keys and values; positions at or past a response's prefix_len hold values that must not be read. Cached positions 0 to prefix_len - 1 of each response are valid. Span positions span_len or more of a response are padding. `row_source`: each group's row holds every number of 0 to 511 once.
All inputs are finite; a program needn't handle non-finite values.
Results may differ from a plain program's by a relative error of at most 0.0045.
Values may be sent and summed in bfloat16 or wider, within the bound.
A program may use at most 64 MiB of HBM per device.

v0:
```python
import math

import jax
import jax.numpy as jnp
from jax import lax
from jax.sharding import PartitionSpec as P


def block_scores(query_rows, key_rows):
    return jnp.einsum("qhd,kd->qhk", query_rows, key_rows, preferred_element_type=jnp.float32) * (
        1.0 / math.sqrt(key_rows.shape[-1])
    )


def block_weights(scores, row_max):
    return lax.optimization_barrier(jnp.exp(scores - row_max[..., None]).astype(jnp.bfloat16))


def cache_scores(query_rows, stored, offset, block_len, valid_len):
    head_dim = query_rows.shape[-1]
    blocks = stored.shape[0] // block_len

    def advance(number, buffer):
        block_rows = lax.dynamic_slice_in_dim(stored, number * block_len, block_len, 0)
        scores = block_scores(query_rows, block_rows[:, :head_dim])
        places = offset + number * block_len + jnp.arange(block_len, dtype=jnp.int32)
        scores = jnp.where((places < valid_len)[None, None, :], scores, -jnp.inf)
        return lax.dynamic_update_slice_in_dim(buffer, scores, number * block_len, 2)

    initial = jnp.full(query_rows.shape[:2] + (stored.shape[0],), -jnp.inf, jnp.float32)
    return lax.fori_loop(0, blocks, advance, initial)


def cache_sums(score_table, stored, block_len, row_max):
    head_dim = stored.shape[-1] // 2
    blocks = stored.shape[0] // block_len

    def advance(number, totals):
        weight_sum, mixture = totals
        block_rows = lax.dynamic_slice_in_dim(stored, number * block_len, block_len, 0)
        scores = lax.dynamic_slice_in_dim(score_table, number * block_len, block_len, 2)
        weights = block_weights(scores, row_max)
        weight_sum = weight_sum + jnp.sum(weights.astype(jnp.float32), axis=-1)
        mixture = mixture + jnp.einsum(
            "qhk,kd->qhd", weights, block_rows[:, head_dim:], preferred_element_type=jnp.float32
        )
        return (weight_sum, mixture)

    initial = (
        jnp.zeros(score_table.shape[:2], jnp.float32),
        jnp.zeros(score_table.shape[:2] + (head_dim,), jnp.float32),
    )
    return lax.fori_loop(0, blocks, advance, initial)


def span_scores(query_rows, fresh_rows):
    head_dim = query_rows.shape[-1]
    scores = block_scores(query_rows, fresh_rows[:, :head_dim])
    row_ids = jnp.arange(query_rows.shape[0], dtype=jnp.int32)
    causal = row_ids[None, :] <= row_ids[:, None]
    return jnp.where(causal[:, None, :], scores, -jnp.inf)


def span_sums(scores, fresh_rows, row_max):
    head_dim = fresh_rows.shape[-1] // 2
    weights = block_weights(scores, row_max)
    weight_sum = jnp.sum(weights.astype(jnp.float32), axis=-1)
    mixture = jnp.einsum(
        "qhk,kd->qhd", weights, fresh_rows[:, head_dim:], preferred_element_type=jnp.float32
    )
    return (weight_sum, mixture)


def finish(weight_sum, mixture, live_count):
    live_rows = jnp.arange(mixture.shape[0], dtype=jnp.int32) < live_count
    return jnp.where(live_rows[:, None, None], mixture / weight_sum[..., None], 0.0).astype(
        jnp.bfloat16
    )


def on_device(queries, span_kv, cache, prefix_len, span_len, row_source):
    kv_heads, group_count, shard_rows, local_heads, head_dim = queries.shape
    responses = cache.shape[0]
    seq_devices = lax.axis_size("seq")
    token_count = shard_rows * seq_devices
    span_rows = token_count // responses
    head_width = local_heads * head_dim
    sent_queries = queries.reshape(kv_heads * group_count, shard_rows, head_width)
    sent_pairs = span_kv.reshape(kv_heads * group_count, shard_rows, 2 * head_dim)
    got_queries, got_pairs = (
        lax.all_to_all(sent_queries, "seq", split_axis=0, concat_axis=1, tiled=True),
        lax.all_to_all(sent_pairs, "seq", split_axis=0, concat_axis=1, tiled=True),
    )
    group_index = lax.axis_index("seq") % group_count
    source_rows = lax.dynamic_index_in_dim(row_source, group_index, 0, keepdims=False)
    query_flat = jnp.take(got_queries[0], source_rows, axis=0)
    query_table = query_flat.reshape(responses, span_rows, local_heads, head_dim)
    pair_table = jnp.take(got_pairs[0], source_rows, axis=0).reshape(
        responses, span_rows, 2 * head_dim
    )
    prefix_here = lax.dynamic_slice_in_dim(prefix_len, group_index * responses, responses)
    span_here = lax.dynamic_slice_in_dim(span_len, group_index * responses, responses)
    stored_all = lax.all_gather(cache, "tp", axis=1, tiled=True)
    block_len = math.gcd(span_rows, stored_all.shape[1])
    own_scores = span_scores(query_table[0], pair_table[0])
    score_table = cache_scores(query_table[0], stored_all[0], 0, block_len, prefix_here[0])
    row_max = jnp.maximum(jnp.max(own_scores, axis=-1), jnp.max(score_table, axis=-1))
    weight_sum, mixture = span_sums(own_scores, pair_table[0], row_max)
    more_sum, more_mix = cache_sums(score_table, stored_all[0], block_len, row_max)
    outputs = [finish(weight_sum + more_sum, mixture + more_mix, span_here[0])]
    attended = jnp.stack(outputs).reshape(1, token_count, head_width)
    returned = lax.all_to_all(attended, "seq", split_axis=1, concat_axis=0, tiled=True)
    return returned.reshape(kv_heads, group_count, shard_rows, local_heads, head_dim)


def solution(mesh):
    in_specs = (
        P(None, None, "seq", "tp", None),
        P(None, None, "seq", None),
        P("seq", "tp", None),
        P(),
        P(),
        P(),
    )
    out_specs = P(None, None, "seq", "tp", None)
    return jax.shard_map(
        on_device, mesh=mesh, in_specs=in_specs, out_specs=out_specs, check_vma=False
    )
```

profile of v0, /device:TPU:2, one launch (start us, length us, event | category | flops | bytes accessed | tf_op | source)
XLA Modules:
  0.0 114.7 jit_solution(3651504552073177956)
XLA Ops:
  6.5 0.0 all-gather.2.cloned.1.call-start
  6.5 0.7 all-gather.2.cloned.1.call-update
  7.3 16.6 %all-to-all-start = ((bf16[64,8,128]{2,1,0:T(8,128)(2,1)}), bf16[64,8,128]{2,1,0:T(8,128)(2,1)S(1)}, u32[]{:S(2)}, u32[]{:S(2)}) async-start(bf16[64,8,128]{2,1,0:T(8,128)(2,1)} %bitcast.78), calls=%async_computation | async-start | bytes 262144 | tf_op jit(solution)/shard_map/all_to_all | solution.py:91
  23.9 1.2 %dynamic_slice.33 = s32[1]{0:T(128)} dynamic-slice(s32[8]{0:T(128)} %param.13, s32[]{:T(128)S(6)} %select_n.89), dynamic_slice_sizes={1} | dynamic-slice | bytes 12 | tf_op jit(solution)/shard_map/dynamic_slice | solution.py:101
  25.1 1.3 %dynamic_slice.31 = s32[1]{0:T(128)} dynamic-slice(s32[8]{0:T(128)} %param.14, s32[]{:T(128)S(6)} %select_n.89), dynamic_slice_sizes={1} | dynamic-slice | bytes 12 | tf_op jit(solution)/shard_map/dynamic_slice | solution.py:102
  26.4 0.7 compare_select_fusion
  27.1 9.5 %all-to-all-done = bf16[64,8,128]{2,1,0:T(8,128)(2,1)S(1)} async-done(((bf16[64,8,128]{2,1,0:T(8,128)(2,1)}), bf16[64,8,128]{2,1,0:T(8,128)(2,1)S(1)}, u32[]{:S(2)}, u32[]{:S(2)}) %all-to-all-start) | async-done | bytes 131104 | tf_op jit(solution)/shard_map/all_to_all | solution.py:91
  36.6 4.6 %all-to-all-start.1 = ((bf16[64,8,256]{2,1,0:T(8,128)(2,1)}), bf16[64,8,256]{2,1,0:T(8,128)(2,1)S(1)}, u32[]{:S(2)}, u32[]{:S(2)}) async-start(bf16[64,8,256]{2,1,0:T(8,128)(2,1)} %bitcast.76), calls=%async_computation.1 | async-start | bytes 524288 | tf_op jit(solution)/shard_map/all_to_all | solution.py:92
  41.2 0.6 iota_compare_fusion.1
  41.9 1.3 %gather_fusion = bf16[512,128]{1,0:T(8,128)(2,1)S(1)} fusion(bf16[512,128]{1,0:T(8,128)(2,1)S(1)} %bitcast.73, s32[1024]{0:T(1024)S(1)} %pad_clamp_fusion), kind=kCustom, calls=%fused_computation | custom fusion | bytes 264192 | tf_op jit(solution)/shard_map/jit(_take)/gather | solution.py:96
  43.2 0.1 bitcast_select_fusion
  43.4 11.8 %all-to-all-done.1 = bf16[64,8,256]{2,1,0:T(8,128)(2,1)S(1)} async-done(((bf16[64,8,256]{2,1,0:T(8,128)(2,1)}), bf16[64,8,256]{2,1,0:T(8,128)(2,1)S(1)}, u32[]{:S(2)}, u32[]{:S(2)}) %all-to-all-start.1) | async-done | bytes 262176 | tf_op jit(solution)/shard_map/all_to_all | solution.py:92
  55.1 1.9 %gather_fusion.1 = bf16[512,256]{1,0:T(8,128)(2,1)S(1)} fusion(bf16[512,256]{1,0:T(8,128)(2,1)S(1)} %bitcast.72, s32[1024]{0:T(1024)S(1)} %pad_clamp_fusion), kind=kCustom, calls=%fused_computation.1 | custom fusion | bytes 526336 | tf_op jit(solution)/shard_map/jit(_take)/gather | solution.py:98
  57.1 0.1 broadcast_select_fusion.1
  57.2 0.0 copy-start
  57.3 0.4 fusion.24
  57.7 0.0 all-gather.2.cloned.1.call-done
  57.7 2.5 %broadcast_in_dim.85 = f32[512,1,2048]{0,2,1:T(8,128)} broadcast(f32[]{:T(128)} %constant.132.clone.1), dimensions={} | broadcast | bytes 4194308 | tf_op jit(solution)/shard_map/broadcast_in_dim | solution.py:30
  60.1 0.0 copy-done
  60.1 11.1 %while.29 = (s32[]{:T(128)}, f32[512,1,2048]{0,2,1:T(8,128)}, s32[]{:T(128)}, bf16[2048,256]{1,0:T(8,128)(2,1)}, bf16[512,1,128]{2,0,1:T(8,128)(2,1)S(1)}, /*index=5*/s32[]{:T(128)}, s32[]{:T(128)}, s32[]{:T(128)}, s32[]{:T(128)}) while((s32[]{:T(128)}, f32[512,1,2048]{0,2,1:T(8,128)}, s32[]{:T(128)}, bf16[2048,256]{1,0:T(8,128)(2,1)}, ...), condition=%wide.region_2.3_spmd, body=%wide.region_1.2_spmd.sunk | while | flops 67634184 | bytes 1312915 | solution.py:31
  60.1 0.5 add_compare_fusion.2
  60.7 2.2 %fusion.34 = f32[512,1,2048]{0,2,1:T(8,128)} fusion(f32[512,1,2048]{0,2,1:T(8,128)} %get-tuple-element.366, s32[]{:T(128)S(6)} %select_n.123, pred[512]{0:T(512)(128)(4,1)S(1)} %add_compare_fusion.2, bf16[2048,256]{1,0:T(8,128)(2,1)} %get-tuple-element.377, bf16[512,1,128]{2,0,1:T(8,128)(2,1)S(1)} %get-tuple-element.378), kind=kOutput, calls=%fused_computation.5.clone.1 | convolution fusion | flops 67633152 | bytes 1312256 | tf_op jit(solution)/shard_map/while/body/eval_jaxpr/qhd,kd->qhk/dot_general | solution.py:10
  62.9 0.5 add_compare_fusion.2
  63.5 2.3 %fusion.34 = f32[512,1,2048]{0,2,1:T(8,128)} fusion(f32[512,1,2048]{0,2,1:T(8,128)} %get-tuple-element.366, s32[]{:T(128)S(6)} %select_n.123, pred[512]{0:T(512)(128)(4,1)S(1)} %add_compare_fusion.2, bf16[2048,256]{1,0:T(8,128)(2,1)} %get-tuple-element.377, bf16[512,1,128]{2,0,1:T(8,128)(2,1)S(1)} %get-tuple-element.378), kind=kOutput, calls=%fused_computation.5.clone.1 | convolution fusion | flops 67633152 | bytes 1312256 | tf_op jit(solution)/shard_map/while/body/eval_jaxpr/qhd,kd->qhk/dot_general | solution.py:10
  65.7 0.5 add_compare_fusion.2
  66.3 2.2 %fusion.34 = f32[512,1,2048]{0,2,1:T(8,128)} fusion(f32[512,1,2048]{0,2,1:T(8,128)} %get-tuple-element.366, s32[]{:T(128)S(6)} %select_n.123, pred[512]{0:T(512)(128)(4,1)S(1)} %add_compare_fusion.2, bf16[2048,256]{1,0:T(8,128)(2,1)} %get-tuple-element.377, bf16[512,1,128]{2,0,1:T(8,128)(2,1)S(1)} %get-tuple-element.378), kind=kOutput, calls=%fused_computation.5.clone.1 | convolution fusion | flops 67633152 | bytes 1312256 | tf_op jit(solution)/shard_map/while/body/eval_jaxpr/qhd,kd->qhk/dot_general | solution.py:10
  68.5 0.5 add_compare_fusion.2
  69.0 2.2 %fusion.34 = f32[512,1,2048]{0,2,1:T(8,128)} fusion(f32[512,1,2048]{0,2,1:T(8,128)} %get-tuple-element.366, s32[]{:T(128)S(6)} %select_n.123, pred[512]{0:T(512)(128)(4,1)S(1)} %add_compare_fusion.2, bf16[2048,256]{1,0:T(8,128)(2,1)} %get-tuple-element.377, bf16[512,1,128]{2,0,1:T(8,128)(2,1)S(1)} %get-tuple-element.378), kind=kOutput, calls=%fused_computation.5.clone.1 | convolution fusion | flops 67633152 | bytes 1312256 | tf_op jit(solution)/shard_map/while/body/eval_jaxpr/qhd,kd->qhk/dot_general | solution.py:10
  71.2 2.5 %reduce_max.19 = f32[512]{0:T(512)S(1)} reduce(f32[512,1,2048]{0,2,1:T(8,128)} %get-tuple-element.386, f32[]{:T(128)} %constant.132.clone.1), dimensions={1,2}, to_apply=%region_3.4 | reduce | flops 1048064 | bytes 4196356 | tf_op jit(solution)/shard_map/reduce_max | solution.py:107
  73.8 0.2 fusion.16
  73.9 0.1 convert_reduce_fusion.1
  74.0 13.1 %while.30 = (s32[]{:T(128)}, f32[512,1]{0,1:T(1,128)S(1)}, f32[512,1,128]{2,0,1:T(8,128)S(1)}, f32[512,1,2048]{0,2,1:T(8,128)}, f32[512,1]{0,1:T(1,128)S(1)}, /*...) while((s32[]{:T(128)}, f32[512,1]{0,1:T(1,128)S(1)}, ...), condition=%wide.region_6.7_spmd.clone, body=%wide.region_4.6_spmd.clone.sunk | while | flops 68289032 | bytes 7481534 | solution.py:53
  74.1 1.3 %constant_dynamic-slice_fusion.4 = f32[512,1,512]{0,2,1:T(8,128)S(1)} fusion(f32[512,1,2048]{0,2,1:T(8,128)} %get-tuple-element.408, s32[]{:T(128)S(6)} %select_n.124), kind=kLoop, calls=%fused_computation.18.clone.1 | loop fusion | bytes 2097156 | tf_op jit(solution)/shard_map/while/body/eval_jaxpr/dynamic_slice | solution.py:41
  75.4 0.3 copy.23
  75.7 0.2 exponential_convert_fusion.3
  75.9 1.2 %fusion.38 = f32[512,1,128]{2,0,1:T(8,128)S(1)} fusion(bf16[512,1,512]{2,0,1:T(8,128)(2,1)S(1)} %exponential_convert_fusion.3, f32[512,1,128]{2,0,1:T(8,128)S(1)} %get-tuple-element.396, bf16[2048,256]{1,0:T(8,128)(2,1)} %get-tuple-element.410, s32[]{:T(128)S(6)} %select_n.124, s32[]{:T(128)S(6)} %add.169, pred[]{:T(512)S(6)} %compare.4), kind=kOutput, calls=%fused_computation.11.clone.1 | convolution fusion | flops 67239936 | bytes 1179657 | tf_op jit(solution)/shard_map/while/body/eval_jaxpr/qhk,kd->qhd/dot_general | solution.py:44
  77.2 0.1 convert_reduce_fusion.3
  77.3 1.3 %constant_dynamic-slice_fusion.4 = f32[512,1,512]{0,2,1:T(8,128)S(1)} fusion(f32[512,1,2048]{0,2,1:T(8,128)} %get-tuple-element.408, s32[]{:T(128)S(6)} %select_n.124), kind=kLoop, calls=%fused_computation.18.clone.1 | loop fusion | bytes 2097156 | tf_op jit(solution)/shard_map/while/body/eval_jaxpr/dynamic_slice | solution.py:41
  78.6 0.3 copy.23
  79.0 0.2 exponential_convert_fusion.3
  79.2 1.2 %fusion.38 = f32[512,1,128]{2,0,1:T(8,128)S(1)} fusion(bf16[512,1,512]{2,0,1:T(8,128)(2,1)S(1)} %exponential_convert_fusion.3, f32[512,1,128]{2,0,1:T(8,128)S(1)} %get-tuple-element.396, bf16[2048,256]{1,0:T(8,128)(2,1)} %get-tuple-element.410, s32[]{:T(128)S(6)} %select_n.124, s32[]{:T(128)S(6)} %add.169, pred[]{:T(512)S(6)} %compare.4), kind=kOutput, calls=%fused_computation.11.clone.1 | convolution fusion | flops 67239936 | bytes 1179657 | tf_op jit(solution)/shard_map/while/body/eval_jaxpr/qhk,kd->qhd/dot_general | solution.py:44
  80.4 0.1 convert_reduce_fusion.3
  80.6 1.3 %constant_dynamic-slice_fusion.4 = f32[512,1,512]{0,2,1:T(8,128)S(1)} fusion(f32[512,1,2048]{0,2,1:T(8,128)} %get-tuple-element.408, s32[]{:T(128)S(6)} %select_n.124), kind=kLoop, calls=%fused_computation.18.clone.1 | loop fusion | bytes 2097156 | tf_op jit(solution)/shard_map/while/body/eval_jaxpr/dynamic_slice | solution.py:41
  81.9 0.3 copy.23
  82.3 0.2 exponential_convert_fusion.3
  82.5 1.2 %fusion.38 = f32[512,1,128]{2,0,1:T(8,128)S(1)} fusion(bf16[512,1,512]{2,0,1:T(8,128)(2,1)S(1)} %exponential_convert_fusion.3, f32[512,1,128]{2,0,1:T(8,128)S(1)} %get-tuple-element.396, bf16[2048,256]{1,0:T(8,128)(2,1)} %get-tuple-element.410, s32[]{:T(128)S(6)} %select_n.124, s32[]{:T(128)S(6)} %add.169, pred[]{:T(512)S(6)} %compare.4), kind=kOutput, calls=%fused_computation.11.clone.1 | convolution fusion | flops 67239936 | bytes 1179657 | tf_op jit(solution)/shard_map/while/body/eval_jaxpr/qhk,kd->qhd/dot_general | solution.py:44
  83.7 0.1 convert_reduce_fusion.3
  83.9 1.3 %constant_dynamic-slice_fusion.4 = f32[512,1,512]{0,2,1:T(8,128)S(1)} fusion(f32[512,1,2048]{0,2,1:T(8,128)} %get-tuple-element.408, s32[]{:T(128)S(6)} %select_n.124), kind=kLoop, calls=%fused_computation.18.clone.1 | loop fusion | bytes 2097156 | tf_op jit(solution)/shard_map/while/body/eval_jaxpr/dynamic_slice | solution.py:41
  85.2 0.3 copy.23
  85.6 0.2 exponential_convert_fusion.3
  85.8 1.2 %fusion.38 = f32[512,1,128]{2,0,1:T(8,128)S(1)} fusion(bf16[512,1,512]{2,0,1:T(8,128)(2,1)S(1)} %exponential_convert_fusion.3, f32[512,1,128]{2,0,1:T(8,128)S(1)} %get-tuple-element.396, bf16[2048,256]{1,0:T(8,128)(2,1)} %get-tuple-element.410, s32[]{:T(128)S(6)} %select_n.124, s32[]{:T(128)S(6)} %add.169, pred[]{:T(512)S(6)} %compare.4), kind=kOutput, calls=%fused_computation.11.clone.1 | convolution fusion | flops 67239936 | bytes 1179657 | tf_op jit(solution)/shard_map/while/body/eval_jaxpr/qhk,kd->qhd/dot_general | solution.py:44
  87.0 0.1 convert_reduce_fusion.3
  87.2 1.3 %fusion.15 = bf16[1,512,128]{2,1,0:T(8,128)(2,1)S(1)} fusion(f32[512,1,128]{2,0,1:T(8,128)S(1)} %get-tuple-element.210, bf16[512,1,512]{0,2,1:T(8,128)(2,1)S(1)} %fusion.16, bf16[512,256]{1,0:T(8,128)(2,1)} %copy-done, f32[512]{0:T(512)S(1)} %bitcast.84, pred[512]{0:T(512)(128)(4,1)S(1)} %iota_compare_fusion.1), kind=kOutput, calls=%fused_computation.26 | convolution fusion | flops 67371008 | bytes 1051136 | tf_op jit(solution)/shard_map/qhk,kd->qhd/dot_general | solution.py:68
  88.5 0.2 copy.21
  88.7 0.5 broadcast.119
  89.2 1.4 %reduce.7 = bf16[512,128]{1,0:T(8,128)(2,1)S(1)} reduce(bf16[512,1,128]{2,1,0:T(2,128)(2,1)S(1)} %bitcast.74, bf16[]{:T(256)} %broadcast.119), dimensions={1}, to_apply=%bitcast.59.reduce_sub_computation | reduce | bytes 262146
  90.6 0.1 reshape.182
  90.7 16.4 %all_to_all.12 = bf16[64,2,512]{2,1,0:T(2,128)(2,1)S(1)} all-to-all(bf16[64,2,512]{2,1,0:T(2,128)(2,1)S(1)} %reshape.182), channel_id=1, replica_groups=mesh['seq'=64,'tp'=8] {'seq'}, dimensions={0} | all-to-all | bytes 262144 | tf_op jit(solution)/shard_map/all_to_all | solution.py:112
  107.1 0.1 reshape.183
  107.2 0.7 copy.19
  (10 shorter events, 0.1 us)
Async XLA Ops:
  6.5 51.1 %all-gather.2.cloned.1.call-start = ((), (), s32[]{:S(2)}) async-start(), calls=%async_computation.3 | async-start | bytes 1179648 | tf_op jit(solution)/shard_map/all_gather | solution.py:103
  7.3 29.3 %all-to-all-start = ((bf16[64,8,128]{2,1,0:T(8,128)(2,1)}), bf16[64,8,128]{2,1,0:T(8,128)(2,1)S(1)}, u32[]{:S(2)}, u32[]{:S(2)}) async-start(bf16[64,8,128]{2,1,0:T(8,128)(2,1)} %bitcast.78), calls=%async_computation | async-start | bytes 262144 | tf_op jit(solution)/shard_map/all_to_all | solution.py:91
  36.6 18.6 %all-to-all-start.1 = ((bf16[64,8,256]{2,1,0:T(8,128)(2,1)}), bf16[64,8,256]{2,1,0:T(8,128)(2,1)S(1)}, u32[]{:S(2)}, u32[]{:S(2)}) async-start(bf16[64,8,256]{2,1,0:T(8,128)(2,1)} %bitcast.76), calls=%async_computation.1 | async-start | bytes 524288 | tf_op jit(solution)/shard_map/all_to_all | solution.py:92
  57.2 2.9 %copy-start = (bf16[512,256]{1,0:T(8,128)(2,1)}, bf16[512,256]{1,0:T(8,128)(2,1)S(1)}, u32[]{:S(2)}) copy-start(bf16[512,256]{1,0:T(8,128)(2,1)S(1)} %broadcast_select_fusion.1) | copy-start | bytes 786436
Sparse Core Ops, SparseCore 0:
  9.5 31.9 all-gather.1
where the time goes:
time: 115 us
  waiting for transfers between devices  22 us (19%)
  starting transfers between devices  21.2 us (18%)
  blocking collectives  16.4 us (14%)
  local copies, waits for them, and re-layouts  16.3 us (14%)
  matrix products  15.4 us (13%)
  between operations  13.6 us (12%)
  other arithmetic  9.57 us (8%)
    all_to_all x1, starting transfers between devices, on_device(): lax.all_to_all(sent_queries, 'seq', split_axis=0, concat_axis=1, tiled=True)  16.6 us
    all_to_all x1, blocking collectives, on_device(): lax.all_to_all(attended, 'seq', split_axis=1, concat_axis=0, tiled=True)  16.4 us
    all_to_all x1, waiting for transfers between devices, on_device(): lax.all_to_all(sent_pairs, 'seq', split_axis=0, concat_axis=1, tiled=True)  11.8 us
    all_to_all x1, waiting for transfers between devices, on_device(): lax.all_to_all(sent_queries, 'seq', split_axis=0, concat_axis=1, tiled=True)  9.46 us
    dot_general x5, matrix products, block_scores(): jnp.einsum('qhd,kd->qhk', query_rows, key_rows, preferred_element_type=jn...  9.26 us
    dynamic_slice x8, local copies, waits for them, and re-layouts, advance(): lax.dynamic_slice_in_dim(score_table, number * block_len, block_len, 2)  6.52 us
    dot_general x4, matrix products, advance(): jnp.einsum('qhk,kd->qhd', weights, block_rows[:, head_dim:], preferred_el...  4.9 us
    all_to_all x1, starting transfers between devices, on_device(): lax.all_to_all(sent_pairs, 'seq', split_axis=0, concat_axis=1, tiled=True)  4.63 us
  transfers between devices with their start and end apart: 3, of which 2 were waited for; matrix products, arithmetic and copies ran while one was open for 7% of the time, Pallas kernels for 0%

commit v1 on v0

v1 whole, which is shorter than its diff:
```python
import functools
import math

import jax
import jax.numpy as jnp
from jax import lax
from jax.experimental import pallas as pl
from jax.experimental.pallas import tpu as pltpu
from jax.sharding import PartitionSpec as P

MESH = pl.DeviceIdType.MESH
SIDE = 8
RING = 4
ROWS = 8
HD = 128
TOK = 512
SHARD = 256
FAR_FIRST = (4, 3, 5, 2, 6, 1, 7)


def kernel(
    q_hbm,
    kv_hbm,
    cache_hbm,
    plen_hbm,
    slen_hbm,
    rs_hbm,
    out_ref,
    q_loc,
    kv_loc,
    q_mid,
    q_all,
    kv_mid,
    kv_all,
    stored,
    plen,
    slen,
    rs,
    pick,
    q_tab,
    m_tab,
    acc_tab,
    att,
    loc_sem,
    send_sem,
    recv_sem,
    ring_send,
    ring_recv,
):
    s = lax.axis_index("seq")
    t = lax.axis_index("tp")
    y, z = s // SIDE, s % SIDE
    x, core = t // 2, t % 2
    other = x * 2 + 1 - core
    right = lax.rem(x + 1, RING) * 2 + core
    left = lax.rem(x + RING - 1, RING) * 2 + core
    x_right, x_left = lax.rem(x + 1, RING), lax.rem(x + RING - 1, RING)
    x_far = lax.rem(x + 2, RING)

    def along_z(d):
        return y * SIDE + lax.rem(z + d, SIDE)

    def along_y(d):
        return lax.rem(y + d, SIDE) * SIDE + z

    barrier = pltpu.get_barrier_semaphore()
    for d in range(1, SIDE):
        pl.semaphore_signal(barrier, inc=1, device_id={"seq": along_z(d)}, device_id_type=MESH)
        pl.semaphore_signal(barrier, inc=1, device_id={"seq": along_y(d)}, device_id_type=MESH)
    for peer in (other, right, left):
        pl.semaphore_signal(barrier, inc=1, device_id={"tp": peer}, device_id_type=MESH)

    half = pl.ds(pl.multiple_of(core * HD, HD), HD)
    loads = [
        pltpu.make_async_copy(q_hbm, q_loc, loc_sem.at[0]),
        pltpu.make_async_copy(kv_hbm.at[:, :, :, half], kv_loc, loc_sem.at[1]),
        pltpu.make_async_copy(cache_hbm, stored.at[pl.ds(t, 1)], loc_sem.at[2]),
        pltpu.make_async_copy(plen_hbm, plen, loc_sem.at[3]),
        pltpu.make_async_copy(slen_hbm, slen, loc_sem.at[4]),
        pltpu.make_async_copy(rs_hbm, rs, loc_sem.at[5]),
    ]
    for load in loads:
        load.start()
    for load in loads:
        load.wait()

    pl.semaphore_wait(barrier, 2 * (SIDE - 1) + 3)

    def push(src, dst, send, recv, **where):
        copy = pltpu.make_async_remote_copy(
            src_ref=src, dst_ref=dst, send_sem=send, recv_sem=recv, device_id=where, device_id_type=MESH
        )
        copy.start()
        return copy

    for d in FAR_FIRST:
        to_z, to_y = lax.rem(z + d, SIDE), lax.rem(y + d, SIDE)
        push(q_loc.at[:, to_z], q_mid.at[z], send_sem.at[0], recv_sem.at[0], seq=along_z(d))
        push(kv_loc.at[to_y], kv_mid.at[y], send_sem.at[1], recv_sem.at[1], seq=along_y(d))
    own_q = pltpu.make_async_copy(q_loc.at[:, z], q_mid.at[z], loc_sem.at[0])
    own_kv = pltpu.make_async_copy(kv_loc.at[y], kv_mid.at[y], loc_sem.at[1])
    own_q.start()
    own_kv.start()

    mine = stored.at[t]
    ring = [
        push(mine, mine, ring_send.at[0], ring_recv.at[0], tp=right),
        push(mine, mine, ring_send.at[1], ring_recv.at[1], tp=left),
        push(mine, mine, ring_send.at[2], ring_recv.at[2], tp=other),
    ]

    source = rs[pl.ds(z, 1), :].astype(jnp.float32)
    source = jnp.broadcast_to(source, (HD, TOK)).T
    lane = lax.broadcasted_iota(jnp.int32, (TOK, HD), 1).astype(jnp.float32)
    row = lax.broadcasted_iota(jnp.int32, (TOK, HD), 0).astype(jnp.float32)
    places = []
    for block in range(TOK // HD):
        hit = source == lane + float(block * HD)
        pick[:, block * HD : (block + 1) * HD] = jnp.where(hit, 1.0, 0.0).astype(jnp.bfloat16)
        places.append(jnp.sum(jnp.where(hit, row, 0.0), axis=0, keepdims=True))
    place = jnp.concatenate(places, axis=1)

    own_q.wait()
    pltpu.make_async_copy(q_mid.at[pl.ds(0, SIDE - 1)], q_mid.at[pl.ds(0, SIDE - 1)], recv_sem.at[0]).wait()
    for d in FAR_FIRST:
        push(q_mid.at[:, lax.rem(y + d, SIDE)], q_all.at[y], send_sem.at[2], recv_sem.at[2], seq=along_y(d))
    own_q = pltpu.make_async_copy(q_mid.at[:, y], q_all.at[y], loc_sem.at[0])
    own_q.start()

    own_kv.wait()
    pltpu.make_async_copy(kv_mid.at[pl.ds(0, SIDE - 1)], kv_mid.at[pl.ds(0, SIDE - 1)], recv_sem.at[1]).wait()
    for d in FAR_FIRST:
        push(
            kv_mid.at[:, lax.rem(z + d, SIDE)], kv_all.at[core, :, z], send_sem.at[3], recv_sem.at[3], seq=along_z(d)
        )
    own_kv = pltpu.make_async_copy(kv_mid.at[:, z], kv_all.at[core, :, z], loc_sem.at[1])
    own_kv.start()

    low, high = pl.ds(0, SHARD // 2), pl.ds(SHARD // 2, SHARD // 2)
    from_left, from_right, from_far = x_left * 2 + core, x_right * 2 + core, x_far * 2 + core
    ring[0].wait_recv()
    ring.append(push(stored.at[from_left, low], stored.at[from_left, low], ring_send.at[3], ring_recv.at[3], tp=right))
    ring.append(push(stored.at[from_left], stored.at[from_left], ring_send.at[4], ring_recv.at[4], tp=other))
    ring[1].wait_recv()
    ring.append(push(stored.at[from_right, high], stored.at[from_right, high], ring_send.at[5], ring_recv.at[5], tp=left))
    ring.append(push(stored.at[from_right], stored.at[from_right], ring_send.at[6], ring_recv.at[6], tp=other))
    ring[3].wait_recv()
    ring[5].wait_recv()
    ring.append(push(stored.at[from_far], stored.at[from_far], ring_send.at[7], ring_recv.at[7], tp=other))
    for step in (2, 4, 6, 7):
        ring[step].wait_recv()

    own_q.wait()
    pltpu.make_async_copy(q_all.at[pl.ds(0, SIDE - 1)], q_all.at[pl.ds(0, SIDE - 1)], recv_sem.at[2]).wait()
    rows_q = q_all[...].reshape(TOK, HD)
    q_tab[...] = jnp.dot(pick[...], rows_q, preferred_element_type=jnp.float32).astype(jnp.bfloat16)

    rate = math.log2(math.e) / math.sqrt(HD)
    contract = (((1,), (1,)), ((), ()))
    block = 128
    keys = RING * 2 * SHARD
    limit = plen[z]

    def cache_block(number, carry):
        rows = pl.ds(pl.multiple_of(number * block, block), block)
        scores = lax.dot_general(
            q_tab[rows, :],
            stored[:, :, :HD].reshape(keys, HD),
            contract,
            preferred_element_type=jnp.float32,
        )
        seen = lax.broadcasted_iota(jnp.int32, (block, keys), 1) < limit
        scores = jnp.where(seen, scores, -jnp.inf)
        top = jnp.max(scores, axis=1, keepdims=True)
        weights = jnp.exp2((scores - top) * rate).astype(jnp.bfloat16)
        values = jnp.concatenate([stored[:, :, HD:].reshape(keys, HD), jnp.ones((keys, HD), jnp.bfloat16)], axis=1)
        acc_tab[rows, :] = jnp.dot(weights, values, preferred_element_type=jnp.float32)
        m_tab[rows, :] = jnp.broadcast_to(top, (block, HD))
        return carry

    lax.fori_loop(0, TOK // block, cache_block, 0)

    own_kv.wait()
    pltpu.make_async_copy(kv_all.at[0, pl.ds(0, SIDE - 1)], kv_all.at[0, pl.ds(0, SIDE - 1)], recv_sem.at[3]).wait()
    swap = push(kv_all.at[core], kv_all.at[core], ring_send.at[8], ring_recv.at[8], tp=other)
    swap.wait_recv()

    live = slen[z]

    def span_block(step, carry):
        number = lax.rem(y // 2 + 2 + step, TOK // block)
        start = pl.multiple_of(number * block, block)
        rows = pl.ds(start, block)
        scores = lax.dot_general(
            q_tab[rows, :], kv_all[0].reshape(TOK, HD), contract, preferred_element_type=jnp.float32
        )
        token = (lax.broadcasted_iota(jnp.int32, (block, TOK), 0) + start).astype(jnp.float32)
        scores = jnp.where(place <= token, scores, -jnp.inf)
        before = m_tab[rows, :][:, :1]
        top = jnp.maximum(before, jnp.max(scores, axis=1, keepdims=True))
        weights = jnp.exp2((scores - top) * rate).astype(jnp.bfloat16)
        values = jnp.concatenate([kv_all[1].reshape(TOK, HD), jnp.ones((TOK, HD), jnp.bfloat16)], axis=1)
        total = acc_tab[rows, :] * jnp.exp2((before - top) * rate)
        total = total + jnp.dot(weights, values, preferred_element_type=jnp.float32)
        result = total[:, :HD] / total[:, HD:]
        token = lax.broadcasted_iota(jnp.int32, (block, HD), 0) + start
        result = jnp.where(token < live, result, 0.0).astype(jnp.bfloat16)
        att[pl.ds(number * (block // ROWS), block // ROWS)] = result.reshape(block // ROWS, ROWS, HD)
        return carry

    def send_block(step, carry):
        number = lax.rem(y // 2 + 2 + step, TOK // block)

        def send_one(i, carry):
            to = number * (block // ROWS) + i

            @pl.when(to != s)
            def _():
                push(att.at[to], out_ref.at[s], send_sem.at[4], recv_sem.at[4], seq=to)

            return carry

        return lax.fori_loop(0, block // ROWS, send_one, carry)

    def both(step, carry):
        span_block(step, carry)
        return send_block(step, carry)

    lax.fori_loop(0, TOK // block, both, 0)
    own = pltpu.make_async_copy(att.at[s], out_ref.at[s], loc_sem.at[0])
    own.start()

    for step in range(8):
        ring[step].wait_send()
    swap.wait_send()
    for stage in range(4):
        pltpu.make_async_copy(q_all.at[pl.ds(0, SIDE - 1)], q_all.at[pl.ds(0, SIDE - 1)], send_sem.at[stage]).wait()
    own.wait()
    peers = SIDE * SIDE - 1
    pltpu.make_async_copy(att.at[pl.ds(0, peers)], att.at[pl.ds(0, peers)], send_sem.at[4]).wait()
    pltpu.make_async_copy(out_ref.at[pl.ds(0, peers)], out_ref.at[pl.ds(0, peers)], recv_sem.at[4]).wait()


def on_device(queries, span_kv, cache, prefix_len, span_len, row_source):
    shape = queries.shape
    hbm = pl.BlockSpec(memory_space=pl.ANY)
    tile = (SIDE, SIDE, ROWS, HD)
    out = pl.pallas_call(
        kernel,
        out_shape=jax.ShapeDtypeStruct((SIDE * SIDE, ROWS, HD), jnp.bfloat16),
        in_specs=[hbm] * 6,
        out_specs=hbm,
        scratch_shapes=[
            pltpu.VMEM(tile, jnp.bfloat16),
            pltpu.VMEM(tile, jnp.bfloat16),
            pltpu.VMEM(tile, jnp.bfloat16),
            pltpu.VMEM(tile, jnp.bfloat16),
            pltpu.VMEM(tile, jnp.bfloat16),
            pltpu.VMEM((2,) + tile, jnp.bfloat16),
            pltpu.VMEM((RING * 2, SHARD, 2 * HD), jnp.bfloat16),
            pltpu.SMEM((8,), jnp.int32),
            pltpu.SMEM((8,), jnp.int32),
            pltpu.VMEM((8, TOK), jnp.int32),
            pltpu.VMEM((TOK, TOK), jnp.bfloat16),
            pltpu.VMEM((TOK, HD), jnp.bfloat16),
            pltpu.VMEM((TOK, HD), jnp.float32),
            pltpu.VMEM((TOK, 2 * HD), jnp.float32),
            pltpu.VMEM((SIDE * SIDE, ROWS, HD), jnp.bfloat16),
            pltpu.SemaphoreType.DMA((6,)),
            pltpu.SemaphoreType.DMA((5,)),
            pltpu.SemaphoreType.DMA((5,)),
            pltpu.SemaphoreType.DMA((9,)),
            pltpu.SemaphoreType.DMA((9,)),
        ],
        compiler_params=pltpu.CompilerParams(collective_id=0, has_side_effects=True),
    )(
        queries.reshape(tile),
        span_kv,
        cache,
        prefix_len,
        span_len,
        row_source,
    )
    return out.reshape(shape)


def solution(mesh):
    in_specs = (
        P(None, None, "seq", "tp", None),
        P(None, None, "seq", None),
        P("seq", "tp", None),
        P(),
        P(),
        P(),
    )
    out_specs = P(None, None, "seq", "tp", None)
    return jax.shard_map(on_device, mesh=mesh, in_specs=in_specs, out_specs=out_specs, check_vma=False)
```

time: 115 us -> 40.4 us (0.35)
  the two profiles are of different devices: /device:TPU:2 before, /device:TPU:1 now
where the time goes in v1:
time: 40.4 us; the launch traced here: 39.8 us
  Pallas kernels  38.2 us (95%)
  local copies, waits for them, and re-layouts  1.57 us (4%)
    pallas_call x1, Pallas kernels, on_device(): pl.pallas_call(kernel, out_shape=jax.ShapeDtypeStruct((SIDE * SIDE, ROWS,...  38.2 us
    unnamed x1, local copies, waits for them, and re-layouts  1.57 us

profile of v1, /device:TPU:1, one launch (start us, length us, event | category | flops | bytes accessed | tf_op | source)
XLA Modules:
  0.0 39.8 jit_solution(12111924921254597859)
XLA Ops:
  0.0 38.2 %shard_map.64 = bf16[64,8,128]{2,1,0:T(8,128)(2,1)} custom-call(bf16[8,8,8,128]{3,2,1,0:T(8,128)(2,1)} %bitcast.5, bf16[8,8,8,256]{3,2,1,0:T(8,128)(2,1)} %kv_hbm.1, bf16[1,256,256]{2,1,0:T(8,128)(2,1)} %cache_hbm.1, s32[8]{0:T(128)} %plen_hbm.1, s32[8]{0:T(128)} %slen_hbm.1, s32[8,512]{1,0:T(8,128)} %rs_hbm.1), custom_call_target="tpu_custom_call" | custom-call | tf_op jit(solution)/shard_map/pallas_call | solution.py:248
  38.2 1.6 %copy.9 = bf16[8,8,8,1,128]{4,2,3,1,0:T(8,128)(2,1)} copy(bf16[8,8,8,1,128]{4,2,3,1,0:T(8,128)(2,1)} %bitcast.4) | data formatting | bytes 262144

commit v2 on v1

v2 whole, which is shorter than its diff:
```python
import functools
import math

import jax
import jax.numpy as jnp
from jax import lax
from jax.experimental import pallas as pl
from jax.experimental.pallas import tpu as pltpu
from jax.sharding import PartitionSpec as P

MESH = pl.DeviceIdType.MESH
SIDE = 8
RING = 4
ROWS = 8
HD = 128
TOK = 512
SHARD = 256
GROUP = 64
FAR_FIRST = (4, 3, 5, 2, 6, 1, 7)
SEND_ORDER = FAR_FIRST + (0,)


def kernel(
    q_hbm,
    kv_hbm,
    cache_hbm,
    plen_hbm,
    slen_hbm,
    rs_hbm,
    out_ref,
    q_mid,
    q_all,
    kv_mid,
    kv_all,
    stored,
    plen,
    slen,
    rs,
    source_tab,
    pick,
    q_tab,
    att,
    loc_sem,
    send_sem,
    recv_sem,
    ring_send,
    ring_recv,
):
    s = lax.axis_index("seq")
    t = lax.axis_index("tp")
    y, z = s // SIDE, s % SIDE
    x, core = t // 2, t % 2
    other = x * 2 + 1 - core
    x_right, x_left, x_far = lax.rem(x + 1, RING), lax.rem(x + RING - 1, RING), lax.rem(x + 2, RING)
    right, left, far = x_right * 2 + core, x_left * 2 + core, x_far * 2 + core
    ys = [lax.rem(y + d, SIDE) for d in range(SIDE)]
    zs = [lax.rem(z + d, SIDE) for d in range(SIDE)]

    barrier = pltpu.get_barrier_semaphore()
    for d in FAR_FIRST:
        pl.semaphore_signal(barrier, inc=1, device_id={"seq": y * SIDE + zs[d]}, device_id_type=MESH)
        pl.semaphore_signal(barrier, inc=1, device_id={"seq": ys[d] * SIDE + z}, device_id_type=MESH)
    for peer in (other, right, left):
        pl.semaphore_signal(barrier, inc=1, device_id={"tp": peer}, device_id_type=MESH)
    with jax.named_scope("W_barrier"):
        pl.semaphore_wait(barrier, 2 * (SIDE - 1) + 3)

    def push(src, dst, send, recv, **where):
        copy = pltpu.make_async_remote_copy(
            src_ref=src, dst_ref=dst, send_sem=send, recv_sem=recv, device_id=where, device_id_type=MESH
        )
        copy.start()
        return copy

    def take(src, dst, sem):
        copy = pltpu.make_async_copy(src, dst, sem)
        copy.start()
        return copy

    def await_all(ref, sem):
        pltpu.make_async_copy(ref, ref, sem).wait()

    half = pl.ds(pl.multiple_of(core * HD, HD), HD)
    for d in FAR_FIRST:
        push(q_hbm.at[:, zs[d]], q_mid.at[z], send_sem.at[0], recv_sem.at[0], seq=y * SIDE + zs[d])
        push(kv_hbm.at[ys[d], :, :, half], kv_mid.at[y], send_sem.at[1], recv_sem.at[1], seq=ys[d] * SIDE + z)
    own_q = take(q_hbm.at[:, z], q_mid.at[z], loc_sem.at[0])
    own_kv = take(kv_hbm.at[y, :, :, half], kv_mid.at[y], loc_sem.at[1])

    shard = cache_hbm.at[0]
    ring = [
        push(shard, stored.at[t], ring_send.at[0], ring_recv.at[0], tp=right),
        push(shard, stored.at[t], ring_send.at[1], ring_recv.at[1], tp=left),
        push(shard, stored.at[t], ring_send.at[2], ring_recv.at[2], tp=other),
    ]
    own_shard = take(shard, stored.at[t], loc_sem.at[2])
    small = [
        take(plen_hbm, plen, loc_sem.at[3]),
        take(slen_hbm, slen, loc_sem.at[4]),
        take(rs_hbm, rs, loc_sem.at[5]),
    ]
    for load in small:
        load.wait()

    source = rs[pl.ds(z, 1), :].astype(jnp.float32)
    source = jnp.broadcast_to(source, (HD, TOK)).T
    source_tab[...] = source
    row = lax.broadcasted_iota(jnp.int32, (TOK, HD), 0).astype(jnp.float32)
    lane = lax.broadcasted_iota(jnp.int32, (TOK, HD), 1).astype(jnp.float32)
    places = [
        jnp.sum(jnp.where(source == lane + float(part * HD), row, 0.0), axis=0, keepdims=True)
        for part in range(TOK // HD)
    ]
    place = jnp.concatenate(places, axis=1)
    lane = lax.broadcasted_iota(jnp.int32, (GROUP, HD), 1).astype(jnp.float32)
    for number, d in enumerate(SEND_ORDER):
        source = source_tab[pl.ds(pl.multiple_of(ys[d] * GROUP, GROUP), GROUP), :]
        for part in range(TOK // HD):
            pick[number * GROUP : (number + 1) * GROUP, part * HD : (part + 1) * HD] = jnp.where(
                source == lane + float(part * HD), 1.0, 0.0
            ).astype(jnp.bfloat16)

    with jax.named_scope("W_q1"):
        own_q.wait()
        await_all(q_mid.at[pl.ds(0, SIDE - 1)], recv_sem.at[0])
    for d in FAR_FIRST:
        push(q_mid.at[:, ys[d]], q_all.at[y], send_sem.at[2], recv_sem.at[2], seq=ys[d] * SIDE + z)
    own_q = take(q_mid.at[:, y], q_all.at[y], loc_sem.at[0])

    with jax.named_scope("W_kv1"):
        own_kv.wait()
        await_all(kv_mid.at[pl.ds(0, SIDE - 1)], recv_sem.at[1])
    for d in FAR_FIRST:
        push(kv_mid.at[:, zs[d]], kv_all.at[core, :, z], send_sem.at[3], recv_sem.at[3], seq=y * SIDE + zs[d])
    own_kv = take(kv_mid.at[:, z], kv_all.at[core, :, z], loc_sem.at[1])

    low, high = pl.ds(0, SHARD // 2), pl.ds(SHARD // 2, SHARD // 2)
    with jax.named_scope("W_ring01"):
        ring[0].wait_recv()
        ring[1].wait_recv()
    ring.append(push(stored.at[left, low], stored.at[left, low], ring_send.at[3], ring_recv.at[3], tp=right))
    ring.append(push(stored.at[right, high], stored.at[right, high], ring_send.at[4], ring_recv.at[4], tp=left))
    ring.append(push(stored.at[left], stored.at[left], ring_send.at[5], ring_recv.at[5], tp=other))
    ring.append(push(stored.at[right], stored.at[right], ring_send.at[6], ring_recv.at[6], tp=other))
    with jax.named_scope("W_ring34"):
        ring[3].wait_recv()
        ring[4].wait_recv()
    ring.append(push(stored.at[far], stored.at[far], ring_send.at[7], ring_recv.at[7], tp=other))

    with jax.named_scope("W_kv2"):
        own_kv.wait()
        await_all(kv_all.at[0, pl.ds(0, SIDE - 1)], recv_sem.at[3])
    swap = push(kv_all.at[core], kv_all.at[core], ring_send.at[8], ring_recv.at[8], tp=other)

    with jax.named_scope("W_q2"):
        own_q.wait()
        await_all(q_all.at[pl.ds(0, SIDE - 1)], recv_sem.at[2])
    with jax.named_scope("C_perm"):
        q_tab[...] = jnp.dot(
            pick[...], q_all[...].reshape(TOK, HD), preferred_element_type=jnp.float32
        ).astype(jnp.bfloat16)
    with jax.named_scope("W_ringall"):
        own_shard.wait()
        for step in (2, 5, 6, 7):
            ring[step].wait_recv()

    rate = math.log2(math.e) / math.sqrt(HD)
    contract = (((1,), (1,)), ((), ()))
    block = 2 * GROUP
    keys = RING * 2 * SHARD
    limit = plen[z]
    live = slen[z]

    def cache_scores(number):
        rows = q_tab[number * block : (number + 1) * block, :]
        scores = lax.dot_general(
            rows, stored[:, :, :HD].reshape(keys, HD), contract, preferred_element_type=jnp.float32
        )
        seen = lax.broadcasted_iota(jnp.int32, (block, keys), 1) < limit
        return jnp.where(seen, scores, -jnp.inf)

    def tokens(number, width):
        first, second = SEND_ORDER[2 * number], SEND_ORDER[2 * number + 1]
        counted = lax.broadcasted_iota(jnp.int32, (GROUP, width), 0)
        return jnp.concatenate([counted + ys[first] * GROUP, counted + ys[second] * GROUP], axis=0)

    def span_scores(number):
        rows = q_tab[number * block : (number + 1) * block, :]
        scores = lax.dot_general(
            rows, kv_all[0].reshape(TOK, HD), contract, preferred_element_type=jnp.float32
        )
        return jnp.where(place <= tokens(number, TOK).astype(jnp.float32), scores, -jnp.inf)

    def attend(number, held, fresh):
        top = jnp.maximum(jnp.max(held, axis=1, keepdims=True), jnp.max(fresh, axis=1, keepdims=True))
        held = jnp.exp2((held - top) * rate).astype(jnp.bfloat16)
        fresh = jnp.exp2((fresh - top) * rate).astype(jnp.bfloat16)
        values = jnp.concatenate([stored[:, :, HD:].reshape(keys, HD), jnp.ones((keys, HD), jnp.bfloat16)], axis=1)
        total = jnp.dot(held, values, preferred_element_type=jnp.float32)
        values = jnp.concatenate([kv_all[1].reshape(TOK, HD), jnp.ones((TOK, HD), jnp.bfloat16)], axis=1)
        total = total + jnp.dot(fresh, values, preferred_element_type=jnp.float32)
        result = total[:, :HD] / total[:, HD:]
        result = jnp.where(tokens(number, HD) < live, result, 0.0).astype(jnp.bfloat16)
        att[2 * number : 2 * number + 2] = result.reshape(2, SIDE, ROWS, HD)
        for piece in (2 * number, 2 * number + 1):
            d = SEND_ORDER[piece]
            for e in SEND_ORDER:
                if d or e:
                    push(
                        att.at[piece, zs[e]],
                        out_ref.at[s],
                        send_sem.at[4],
                        recv_sem.at[4],
                        seq=ys[d] * SIDE + zs[e],
                    )

    with jax.named_scope("C_cache0"):
        held = cache_scores(0)
    with jax.named_scope("W_swap"):
        swap.wait_recv()
    fresh = span_scores(0)
    for number in range(TOK // block):
        with jax.named_scope(f"C_block{number}"):
            last = number == TOK // block - 1
            following = None if last else (cache_scores(number + 1), span_scores(number + 1))
            attend(number, held, fresh)
            if not last:
                held, fresh = following
    own = take(att.at[SIDE - 1, z], out_ref.at[s], loc_sem.at[0])

    for step in range(8):
        ring[step].wait_send()
    swap.wait_send()
    for stage in range(4):
        await_all(q_all.at[pl.ds(0, SIDE - 1)], send_sem.at[stage])
    own.wait()
    peers = pl.ds(0, SIDE * SIDE - 1)
    with jax.named_scope("W_outsend"):
        await_all(out_ref.at[peers], send_sem.at[4])
    with jax.named_scope("W_out"):
        await_all(out_ref.at[peers], recv_sem.at[4])


def on_device(queries, span_kv, cache, prefix_len, span_len, row_source):
    shape = queries.shape
    hbm = pl.BlockSpec(memory_space=pl.ANY)
    tile = (SIDE, SIDE, ROWS, HD)
    out = pl.pallas_call(
        kernel,
        out_shape=jax.ShapeDtypeStruct((SIDE * SIDE, ROWS, HD), jnp.bfloat16),
        in_specs=[hbm] * 6,
        out_specs=pl.BlockSpec(memory_space=pltpu.VMEM),
        scratch_shapes=[
            pltpu.VMEM(tile, jnp.bfloat16),
            pltpu.VMEM(tile, jnp.bfloat16),
            pltpu.VMEM(tile, jnp.bfloat16),
            pltpu.VMEM((2,) + tile, jnp.bfloat16),
            pltpu.VMEM((RING * 2, SHARD, 2 * HD), jnp.bfloat16),
            pltpu.SMEM((8,), jnp.int32),
            pltpu.SMEM((8,), jnp.int32),
            pltpu.VMEM((8, TOK), jnp.int32),
            pltpu.VMEM((TOK, HD), jnp.float32),
            pltpu.VMEM((TOK, TOK), jnp.bfloat16),
            pltpu.VMEM((TOK, HD), jnp.bfloat16),
            pltpu.VMEM(tile, jnp.bfloat16),
            pltpu.SemaphoreType.DMA((6,)),
            pltpu.SemaphoreType.DMA((5,)),
            pltpu.SemaphoreType.DMA((5,)),
            pltpu.SemaphoreType.DMA((9,)),
            pltpu.SemaphoreType.DMA((9,)),
        ],
        compiler_params=pltpu.CompilerParams(collective_id=0, has_side_effects=True),
    )(
        queries.reshape(tile),
        span_kv,
        cache,
        prefix_len,
        span_len,
        row_source,
    )
    return out.reshape(shape)


def solution(mesh):
    in_specs = (
        P(None, None, "seq", "tp", None),
        P(None, None, "seq", None),
        P("seq", "tp", None),
        P(),
        P(),
        P(),
    )
    out_specs = P(None, None, "seq", "tp", None)
    return jax.shard_map(on_device, mesh=mesh, in_specs=in_specs, out_specs=out_specs, check_vma=False)
```

time: 40.4 us -> 37.3 us (0.923)
  Pallas kernels: 38.2 us -> 35.5 us
    pallas_call x1, Pallas kernels: 38.2 us -> 35.5 us  [on_device(): pl.pallas_call(kernel, out_shape=jax.ShapeDtypeStruct((SIDE * SIDE, ROWS,...]
where the time goes in v2:
time: 37.3 us; the launch traced here: 37.1 us
  Pallas kernels  35.5 us (95%)
  local copies, waits for them, and re-layouts  1.57 us (4%)
    pallas_call x1, Pallas kernels, on_device(): pl.pallas_call(kernel, out_shape=jax.ShapeDtypeStruct((SIDE * SIDE, ROWS,...  35.5 us
    unnamed x1, local copies, waits for them, and re-layouts  1.57 us

profile of v2, /device:TPU:1, one launch (start us, length us, event | category | flops | bytes accessed | tf_op | source)
XLA Modules:
  0.0 37.1 jit_solution(9320697989714609213)
XLA Ops:
  0.0 35.5 %shard_map.64 = bf16[64,8,128]{2,1,0:T(8,128)(2,1)} custom-call(bf16[8,8,8,128]{3,2,1,0:T(8,128)(2,1)} %bitcast.5, bf16[8,8,8,256]{3,2,1,0:T(8,128)(2,1)} %kv_hbm.1, bf16[1,256,256]{2,1,0:T(8,128)(2,1)} %cache_hbm.1, s32[8]{0:T(128)} %plen_hbm.1, s32[8]{0:T(128)} %slen_hbm.1, s32[8,512]{1,0:T(8,128)} %rs_hbm.1), custom_call_target="tpu_custom_call" | custom-call | tf_op jit(solution)/shard_map/pallas_call | solution.py:248
  35.5 1.6 %copy.9 = bf16[8,8,8,1,128]{4,2,3,1,0:T(8,128)(2,1)} copy(bf16[8,8,8,1,128]{4,2,3,1,0:T(8,128)(2,1)} %bitcast.4) | data formatting | bytes 262144

commit v3 on v2

--- a/solution.py
+++ b/solution.py
@@ -120,20 +120,6 @@
                 source == lane + float(part * HD), 1.0, 0.0
             ).astype(jnp.bfloat16)
 
-    with jax.named_scope("W_q1"):
-        own_q.wait()
-        await_all(q_mid.at[pl.ds(0, SIDE - 1)], recv_sem.at[0])
-    for d in FAR_FIRST:
-        push(q_mid.at[:, ys[d]], q_all.at[y], send_sem.at[2], recv_sem.at[2], seq=ys[d] * SIDE + z)
-    own_q = take(q_mid.at[:, y], q_all.at[y], loc_sem.at[0])
-
-    with jax.named_scope("W_kv1"):
-        own_kv.wait()
-        await_all(kv_mid.at[pl.ds(0, SIDE - 1)], recv_sem.at[1])
-    for d in FAR_FIRST:
-        push(kv_mid.at[:, zs[d]], kv_all.at[core, :, z], send_sem.at[3], recv_sem.at[3], seq=y * SIDE + zs[d])
-    own_kv = take(kv_mid.at[:, z], kv_all.at[core, :, z], loc_sem.at[1])
-
     low, high = pl.ds(0, SHARD // 2), pl.ds(SHARD // 2, SHARD // 2)
     with jax.named_scope("W_ring01"):
         ring[0].wait_recv()
@@ -142,6 +128,21 @@
     ring.append(push(stored.at[right, high], stored.at[right, high], ring_send.at[4], ring_recv.at[4], tp=left))
     ring.append(push(stored.at[left], stored.at[left], ring_send.at[5], ring_recv.at[5], tp=other))
     ring.append(push(stored.at[right], stored.at[right], ring_send.at[6], ring_recv.at[6], tp=other))
+
+    with jax.named_scope("W_q1"):
+        own_q.wait()
+        await_all(q_mid.at[pl.ds(0, SIDE - 1)], recv_sem.at[0])
+    for d in FAR_FIRST:
+        push(q_mid.at[:, ys[d]], q_all.at[y], send_sem.at[2], recv_sem.at[2], seq=ys[d] * SIDE + z)
+    own_q = take(q_mid.at[:, y], q_all.at[y], loc_sem.at[0])
+
+    with jax.named_scope("W_kv1"):
+        own_kv.wait()
+        await_all(kv_mid.at[pl.ds(0, SIDE - 1)], recv_sem.at[1])
+    for d in FAR_FIRST:
+        push(kv_mid.at[:, zs[d]], kv_all.at[core, :, z], send_sem.at[3], recv_sem.at[3], seq=y * SIDE + zs[d])
+    own_kv = take(kv_mid.at[:, z], kv_all.at[core, :, z], loc_sem.at[1])
+
     with jax.named_scope("W_ring34"):
         ring[3].wait_recv()
         ring[4].wait_recv()
@@ -155,10 +156,6 @@
     with jax.named_scope("W_q2"):
         own_q.wait()
         await_all(q_all.at[pl.ds(0, SIDE - 1)], recv_sem.at[2])
-    with jax.named_scope("C_perm"):
-        q_tab[...] = jnp.dot(
-            pick[...], q_all[...].reshape(TOK, HD), preferred_element_type=jnp.float32
-        ).astype(jnp.bfloat16)
     with jax.named_scope("W_ringall"):
         own_shard.wait()
         for step in (2, 5, 6, 7):
@@ -172,9 +169,12 @@
     live = slen[z]
 
     def cache_scores(number):
-        rows = q_tab[number * block : (number + 1) * block, :]
+        rows = slice(number * block, (number + 1) * block)
+        rows_q = jnp.dot(pick[rows, :], q_all[...].reshape(TOK, HD), preferred_element_type=jnp.float32)
+        rows_q = rows_q.astype(jnp.bfloat16)
+        q_tab[rows, :] = rows_q
         scores = lax.dot_general(
-            rows, stored[:, :, :HD].reshape(keys, HD), contract, preferred_element_type=jnp.float32
+            rows_q, stored[:, :, :HD].reshape(keys, HD), contract, preferred_element_type=jnp.float32
         )
         seen = lax.broadcasted_iota(jnp.int32, (block, keys), 1) < limit
         return jnp.where(seen, scores, -jnp.inf)
@@ -247,7 +247,7 @@
     tile = (SIDE, SIDE, ROWS, HD)
     out = pl.pallas_call(
         kernel,
-        out_shape=jax.ShapeDtypeStruct((SIDE * SIDE, ROWS, HD), jnp.bfloat16),
+        out_shape=pltpu.VMEM((SIDE * SIDE, ROWS, HD), jnp.bfloat16),
         in_specs=[hbm] * 6,
         out_specs=pl.BlockSpec(memory_space=pltpu.VMEM),
         scratch_shapes=[

time: 37.3 us -> 36 us (0.965)
  local copies, waits for them, and re-layouts: 1.57 us -> 0.66 us
    unnamed x1, local copies, waits for them, and re-layouts: 1.57 us -> 0.66 us
where the time goes in v3:
time: 36 us; the launch traced here: 35.9 us
  Pallas kernels  35.2 us (98%)
  local copies, waits for them, and re-layouts  0.66 us (2%)
    pallas_call x1, Pallas kernels, on_device(): pl.pallas_call(kernel, out_shape=pltpu.VMEM((SIDE * SIDE, ROWS, HD), jnp....  35.2 us

profile of v3, /device:TPU:1, one launch (start us, length us, event | category | flops | bytes accessed | tf_op | source)
XLA Modules:
  0.0 35.9 jit_solution(8053944781507330231)
XLA Ops:
  0.0 35.2 %shard_map.64 = bf16[64,8,128]{2,1,0:T(8,128)(2,1)S(1)} custom-call(bf16[8,8,8,128]{3,2,1,0:T(8,128)(2,1)} %bitcast.5, bf16[8,8,8,256]{3,2,1,0:T(8,128)(2,1)} %kv_hbm.1, bf16[1,256,256]{2,1,0:T(8,128)(2,1)} %cache_hbm.1, s32[8]{0:T(128)} %plen_hbm.1, s32[8]{0:T(128)} %slen_hbm.1, s32[8,512]{1,0:T(8,128)} %rs_hbm.1), custom_call_target="tpu_custom_call" | custom-call | tf_op jit(solution)/shard_map/pallas_call | solution.py:248
  35.2 0.7 %copy.9 = bf16[8,8,8,1,128]{4,2,3,1,0:T(8,128)(2,1)} copy(bf16[8,8,8,1,128]{4,2,3,1,0:T(8,128)(2,1)S(1)} %bitcast.4) | data formatting | bytes 262144

commit v4 on v3

--- a/solution.py
+++ b/solution.py
@@ -17,7 +17,7 @@
 SHARD = 256
 GROUP = 64
 FAR_FIRST = (4, 3, 5, 2, 6, 1, 7)
-SEND_ORDER = FAR_FIRST + (0,)
+Y_ORDER = (0, 1, 2, 3, 7, 6, 5, 4)
 
 
 def kernel(
@@ -36,13 +36,15 @@
     plen,
     slen,
     rs,
-    source_tab,
     pick,
     q_tab,
     att,
+    known_y,
+    known_z,
     loc_sem,
     send_sem,
     recv_sem,
+    piece_sem,
     ring_send,
     ring_recv,
 ):
@@ -56,14 +58,22 @@
     ys = [lax.rem(y + d, SIDE) for d in range(SIDE)]
     zs = [lax.rem(z + d, SIDE) for d in range(SIDE)]
 
+    rank = jnp.where(y < SIDE // 2, y, SIDE + SIDE // 2 - 1 - y)
+
+    def signal(semaphore, **where):
+        pl.semaphore_signal(semaphore, inc=1, device_id=where, device_id_type=MESH)
+
     barrier = pltpu.get_barrier_semaphore()
-    for d in FAR_FIRST:
-        pl.semaphore_signal(barrier, inc=1, device_id={"seq": y * SIDE + zs[d]}, device_id_type=MESH)
-        pl.semaphore_signal(barrier, inc=1, device_id={"seq": ys[d] * SIDE + z}, device_id_type=MESH)
     for peer in (other, right, left):
-        pl.semaphore_signal(barrier, inc=1, device_id={"tp": peer}, device_id_type=MESH)
+        signal(barrier, tp=peer)
+    for step in range(1, SIDE):
+        pl.when(step > z)(functools.partial(signal, barrier, seq=y * SIDE + step))
+        pl.when(step > rank)(functools.partial(signal, barrier, seq=Y_ORDER[step] * SIDE + z))
     with jax.named_scope("W_barrier"):
-        pl.semaphore_wait(barrier, 2 * (SIDE - 1) + 3)
+        pl.semaphore_wait(barrier, z + rank + 3)
+    for step in range(SIDE - 1):
+        pl.when(step < z)(functools.partial(signal, known_z.at[z], seq=y * SIDE + step))
+        pl.when(step < rank)(functools.partial(signal, known_y.at[rank], seq=Y_ORDER[step] * SIDE + z))
 
     def push(src, dst, send, recv, **where):
         copy = pltpu.make_async_remote_copy(
@@ -80,12 +90,28 @@
     def await_all(ref, sem):
         pltpu.make_async_copy(ref, ref, sem).wait()
 
-    half = pl.ds(pl.multiple_of(core * HD, HD), HD)
-    for d in FAR_FIRST:
-        push(q_hbm.at[:, zs[d]], q_mid.at[z], send_sem.at[0], recv_sem.at[0], seq=y * SIDE + zs[d])
-        push(kv_hbm.at[ys[d], :, :, half], kv_mid.at[y], send_sem.at[1], recv_sem.at[1], seq=ys[d] * SIDE + z)
+    mover = core == 1
+
+    def send_q(to):
+        push(q_hbm.at[:, to], q_mid.at[z], send_sem.at[0], recv_sem.at[0], seq=y * SIDE + to)
+
+    def send_kv(to):
+        push(kv_hbm.at[to], kv_mid.at[y], send_sem.at[1], recv_sem.at[1], seq=to * SIDE + z)
+
+    def send_q_known(to):
+        pl.semaphore_wait(known_z.at[to], 1)
+        send_q(to)
+
+    def send_kv_known(step):
+        pl.semaphore_wait(known_y.at[step], 1)
+        send_kv(Y_ORDER[step])
+
+    for step in range(SIDE - 1):
+        pl.when(step < z)(functools.partial(send_q, step))
+        pl.when(jnp.logical_and(step < rank, mover))(functools.partial(send_kv, Y_ORDER[step]))
     own_q = take(q_hbm.at[:, z], q_mid.at[z], loc_sem.at[0])
-    own_kv = take(kv_hbm.at[y, :, :, half], kv_mid.at[y], loc_sem.at[1])
+    own_kv = pltpu.make_async_copy(kv_hbm.at[y], kv_mid.at[y], loc_sem.at[1])
+    pl.when(mover)(own_kv.start)
 
     shard = cache_hbm.at[0]
     ring = [
@@ -104,7 +130,6 @@
 
     source = rs[pl.ds(z, 1), :].astype(jnp.float32)
     source = jnp.broadcast_to(source, (HD, TOK)).T
-    source_tab[...] = source
     row = lax.broadcasted_iota(jnp.int32, (TOK, HD), 0).astype(jnp.float32)
     lane = lax.broadcasted_iota(jnp.int32, (TOK, HD), 1).astype(jnp.float32)
     places = [
@@ -112,13 +137,21 @@
         for part in range(TOK // HD)
     ]
     place = jnp.concatenate(places, axis=1)
-    lane = lax.broadcasted_iota(jnp.int32, (GROUP, HD), 1).astype(jnp.float32)
-    for number, d in enumerate(SEND_ORDER):
-        source = source_tab[pl.ds(pl.multiple_of(ys[d] * GROUP, GROUP), GROUP), :]
-        for part in range(TOK // HD):
-            pick[number * GROUP : (number + 1) * GROUP, part * HD : (part + 1) * HD] = jnp.where(
-                source == lane + float(part * HD), 1.0, 0.0
-            ).astype(jnp.bfloat16)
+    source = jnp.swapaxes(source.reshape(SIDE, SIDE, ROWS, HD), 0, 1).reshape(TOK, HD)
+    for part in range(TOK // HD):
+        pick[:, part * HD : (part + 1) * HD] = jnp.where(source == lane + float(part * HD), 1.0, 0.0).astype(
+            jnp.bfloat16
+        )
+
+    with jax.named_scope("W_upper"):
+        for step in range(1, SIDE):
+            pl.when(jnp.logical_and(step > rank, mover))(functools.partial(send_kv_known, step))
+        for step in range(1, SIDE):
+            pl.when(step > z)(functools.partial(send_q_known, step))
+        for step in range(1, SIDE):
+            pl.when(jnp.logical_and(step > rank, jnp.logical_not(mover)))(
+                functools.partial(pl.semaphore_wait, known_y.at[step], 1)
+            )
 
     low, high = pl.ds(0, SHARD // 2), pl.ds(SHARD // 2, SHARD // 2)
     with jax.named_scope("W_ring01"):
@@ -129,6 +162,18 @@
     ring.append(push(stored.at[left], stored.at[left], ring_send.at[5], ring_recv.at[5], tp=other))
     ring.append(push(stored.at[right], stored.at[right], ring_send.at[6], ring_recv.at[6], tp=other))
 
+    own_pair = pltpu.make_async_copy(kv_mid.at[:, z], kv_all.at[:, z], loc_sem.at[1])
+
+    def spread_span():
+        with jax.named_scope("W_kv1"):
+            own_kv.wait()
+            await_all(kv_mid.at[pl.ds(0, SIDE - 1)], recv_sem.at[1])
+        for d in FAR_FIRST:
+            push(kv_mid.at[:, zs[d]], kv_all.at[:, z], send_sem.at[3], piece_sem.at[z], seq=y * SIDE + zs[d])
+        own_pair.start()
+
+    pl.when(mover)(spread_span)
+
     with jax.named_scope("W_q1"):
         own_q.wait()
         await_all(q_mid.at[pl.ds(0, SIDE - 1)], recv_sem.at[0])
@@ -136,22 +181,20 @@
         push(q_mid.at[:, ys[d]], q_all.at[y], send_sem.at[2], recv_sem.at[2], seq=ys[d] * SIDE + z)
     own_q = take(q_mid.at[:, y], q_all.at[y], loc_sem.at[0])
 
-    with jax.named_scope("W_kv1"):
-        own_kv.wait()
-        await_all(kv_mid.at[pl.ds(0, SIDE - 1)], recv_sem.at[1])
-    for d in FAR_FIRST:
-        push(kv_mid.at[:, zs[d]], kv_all.at[core, :, z], send_sem.at[3], recv_sem.at[3], seq=y * SIDE + zs[d])
-    own_kv = take(kv_mid.at[:, z], kv_all.at[core, :, z], loc_sem.at[1])
-
     with jax.named_scope("W_ring34"):
         ring[3].wait_recv()
         ring[4].wait_recv()
     ring.append(push(stored.at[far], stored.at[far], ring_send.at[7], ring_recv.at[7], tp=other))
 
-    with jax.named_scope("W_kv2"):
-        own_kv.wait()
-        await_all(kv_all.at[0, pl.ds(0, SIDE - 1)], recv_sem.at[3])
-    swap = push(kv_all.at[core], kv_all.at[core], ring_send.at[8], ring_recv.at[8], tp=other)
+    def hand_over():
+        for step in range(SIDE):
+            piece = kv_all.at[:, step]
+            with jax.named_scope("W_kv2"):
+                pl.when(step == z)(own_pair.wait)
+                pl.when(step != z)(functools.partial(await_all, piece, piece_sem.at[step]))
+            push(piece, piece, send_sem.at[5], recv_sem.at[3], tp=other)
+
+    pl.when(mover)(hand_over)
 
     with jax.named_scope("W_q2"):
         own_q.wait()
@@ -180,16 +223,21 @@
         return jnp.where(seen, scores, -jnp.inf)
 
     def tokens(number, width):
-        first, second = SEND_ORDER[2 * number], SEND_ORDER[2 * number + 1]
-        counted = lax.broadcasted_iota(jnp.int32, (GROUP, width), 0)
-        return jnp.concatenate([counted + ys[first] * GROUP, counted + ys[second] * GROUP], axis=0)
+        count = lax.broadcasted_iota(jnp.int32, (block, width), 0)
+        in_group = lax.bitwise_and(count, GROUP - 1)
+        return (in_group - lax.bitwise_and(in_group, ROWS - 1)) * SIDE + (
+            lax.bitwise_and(in_group, ROWS - 1) + ((count - in_group) // SIDE + 2 * number * ROWS)
+        )
 
     def span_scores(number):
         rows = q_tab[number * block : (number + 1) * block, :]
         scores = lax.dot_general(
-            rows, kv_all[0].reshape(TOK, HD), contract, preferred_element_type=jnp.float32
+            rows, kv_all[:, :, :, :HD].reshape(TOK, HD), contract, preferred_element_type=jnp.float32
         )
         return jnp.where(place <= tokens(number, TOK).astype(jnp.float32), scores, -jnp.inf)
+
+    def send_out(to, d):
+        push(att.at[to, ys[d]], out_ref.at[s], send_sem.at[4], recv_sem.at[4], seq=ys[d] * SIDE + to)
 
     def attend(number, held, fresh):
         top = jnp.maximum(jnp.max(held, axis=1, keepdims=True), jnp.max(fresh, axis=1, keepdims=True))
@@ -197,27 +245,20 @@
         fresh = jnp.exp2((fresh - top) * rate).astype(jnp.bfloat16)
         values = jnp.concatenate([stored[:, :, HD:].reshape(keys, HD), jnp.ones((keys, HD), jnp.bfloat16)], axis=1)
         total = jnp.dot(held, values, preferred_element_type=jnp.float32)
-        values = jnp.concatenate([kv_all[1].reshape(TOK, HD), jnp.ones((TOK, HD), jnp.bfloat16)], axis=1)
+        values = jnp.concatenate([kv_all[:, :, :, HD:].reshape(TOK, HD), jnp.ones((TOK, HD), jnp.bfloat16)], axis=1)
         total = total + jnp.dot(fresh, values, preferred_element_type=jnp.float32)
         result = total[:, :HD] / total[:, HD:]
         result = jnp.where(tokens(number, HD) < live, result, 0.0).astype(jnp.bfloat16)
         att[2 * number : 2 * number + 2] = result.reshape(2, SIDE, ROWS, HD)
-        for piece in (2 * number, 2 * number + 1):
-            d = SEND_ORDER[piece]
-            for e in SEND_ORDER:
-                if d or e:
-                    push(
-                        att.at[piece, zs[e]],
-                        out_ref.at[s],
-                        send_sem.at[4],
-                        recv_sem.at[4],
-                        seq=ys[d] * SIDE + zs[e],
-                    )
+        for to in (2 * number, 2 * number + 1):
+            for d in FAR_FIRST:
+                send_out(to, d)
+            pl.when(to != z)(functools.partial(send_out, to, 0))
 
     with jax.named_scope("C_cache0"):
         held = cache_scores(0)
     with jax.named_scope("W_swap"):
-        swap.wait_recv()
+        pl.when(jnp.logical_not(mover))(functools.partial(await_all, kv_all, recv_sem.at[3]))
     fresh = span_scores(0)
     for number in range(TOK // block):
         with jax.named_scope(f"C_block{number}"):
@@ -226,13 +267,18 @@
             attend(number, held, fresh)
             if not last:
                 held, fresh = following
-    own = take(att.at[SIDE - 1, z], out_ref.at[s], loc_sem.at[0])
+    own = take(att.at[z, y], out_ref.at[s], loc_sem.at[0])
 
     for step in range(8):
         ring[step].wait_send()
-    swap.wait_send()
-    for stage in range(4):
-        await_all(q_all.at[pl.ds(0, SIDE - 1)], send_sem.at[stage])
+    def span_sent():
+        await_all(kv_all, send_sem.at[5])
+        await_all(kv_mid.at[pl.ds(0, SIDE - 1)], send_sem.at[1])
+        await_all(kv_mid.at[pl.ds(0, SIDE - 1)], send_sem.at[3])
+
+    pl.when(mover)(span_sent)
+    await_all(q_all.at[pl.ds(0, SIDE - 1)], send_sem.at[0])
+    await_all(q_all.at[pl.ds(0, SIDE - 1)], send_sem.at[2])
     own.wait()
     peers = pl.ds(0, SIDE * SIDE - 1)
     with jax.named_scope("W_outsend"):
@@ -253,21 +299,23 @@
         scratch_shapes=[
             pltpu.VMEM(tile, jnp.bfloat16),
             pltpu.VMEM(tile, jnp.bfloat16),
-            pltpu.VMEM(tile, jnp.bfloat16),
-            pltpu.VMEM((2,) + tile, jnp.bfloat16),
+            pltpu.VMEM((SIDE, SIDE, ROWS, 2 * HD), jnp.bfloat16),
+            pltpu.VMEM((SIDE, SIDE, ROWS, 2 * HD), jnp.bfloat16),
             pltpu.VMEM((RING * 2, SHARD, 2 * HD), jnp.bfloat16),
             pltpu.SMEM((8,), jnp.int32),
             pltpu.SMEM((8,), jnp.int32),
             pltpu.VMEM((8, TOK), jnp.int32),
-            pltpu.VMEM((TOK, HD), jnp.float32),
             pltpu.VMEM((TOK, TOK), jnp.bfloat16),
             pltpu.VMEM((TOK, HD), jnp.bfloat16),
             pltpu.VMEM(tile, jnp.bfloat16),
+            pltpu.SemaphoreType.REGULAR((SIDE,)),
+            pltpu.SemaphoreType.REGULAR((SIDE,)),
+            pltpu.SemaphoreType.DMA((6,)),
             pltpu.SemaphoreType.DMA((6,)),
             pltpu.SemaphoreType.DMA((5,)),
-            pltpu.SemaphoreType.DMA((5,)),
-            pltpu.SemaphoreType.DMA((9,)),
-            pltpu.SemaphoreType.DMA((9,)),
+            pltpu.SemaphoreType.DMA((SIDE,)),
+            pltpu.SemaphoreType.DMA((8,)),
+            pltpu.SemaphoreType.DMA((8,)),
         ],
         compiler_params=pltpu.CompilerParams(collective_id=0, has_side_effects=True),
     )(

time: 36 us -> 35 us (0.972)
  the two profiles are of different devices: /device:TPU:1 before, /device:TPU:8 now
where the time goes in v4:
time: 35 us; the launch traced here: 34.9 us
  Pallas kernels  34.2 us (98%)
  local copies, waits for them, and re-layouts  0.66 us (2%)
    pallas_call x1, Pallas kernels, on_device(): pl.pallas_call(kernel, out_shape=pltpu.VMEM((SIDE * SIDE, ROWS, HD), jnp....  34.2 us

profile of v4, /device:TPU:8, one launch (start us, length us, event | category | flops | bytes accessed | tf_op | source)
XLA Modules:
  0.0 34.9 jit_solution(6464940209540830102)
XLA Ops:
  0.0 34.2 %shard_map.64 = bf16[64,8,128]{2,1,0:T(8,128)(2,1)S(1)} custom-call(bf16[8,8,8,128]{3,2,1,0:T(8,128)(2,1)} %bitcast.5, bf16[8,8,8,256]{3,2,1,0:T(8,128)(2,1)} %kv_hbm.1, bf16[1,256,256]{2,1,0:T(8,128)(2,1)} %cache_hbm.1, s32[8]{0:T(128)} %plen_hbm.1, s32[8]{0:T(128)} %slen_hbm.1, s32[8,512]{1,0:T(8,128)} %rs_hbm.1), custom_call_target="tpu_custom_call" | custom-call | tf_op jit(solution)/shard_map/pallas_call | solution.py:294
  34.2 0.7 %copy.9 = bf16[8,8,8,1,128]{4,2,3,1,0:T(8,128)(2,1)} copy(bf16[8,8,8,1,128]{4,2,3,1,0:T(8,128)(2,1)S(1)} %bitcast.4) | data formatting | bytes 262144

commit v5 on v4

v5 whole, which is shorter than its diff:
```python
import functools
import math

import jax
import jax.numpy as jnp
from jax import lax
from jax.experimental import pallas as pl
from jax.experimental.pallas import tpu as pltpu
from jax.sharding import PartitionSpec as P

MESH = pl.DeviceIdType.MESH
SIDE = 8
RING = 4
ROWS = 8
HD = 128
TOK = 512
SHARD = 256
EARLY = 4
GROUP = 64
FAR_FIRST = (4, 3, 5, 2, 6, 1, 7)
BLOCKS = ((0, 2), (2, 4), (4, 6), (6, 8))
Y_ORDER = (0, 1, 2, 3, 7, 6, 5, 4)


def kernel(
    q_hbm,
    kv_hbm,
    cache_hbm,
    plen_hbm,
    slen_hbm,
    rs_hbm,
    out_ref,
    q_mid,
    q_up,
    q_all,
    kv_mid,
    kv_up,
    kv_all,
    stored,
    plen,
    slen,
    rs,
    pick,
    q_tab,
    att,
    known_y,
    known_z,
    q_bytes,
    loc_sem,
    z_send,
    z_recv,
    up_send,
    up_recv,
    y_send,
    far_send,
    q_done,
    low_done,
    high_done,
    swap_send,
    swap_recv,
    out_send,
    out_recv,
    ring_send,
    ring_recv,
):
    s = lax.axis_index("seq")
    t = lax.axis_index("tp")
    y, z = s // SIDE, s % SIDE
    x, core = t // 2, t % 2
    other = x * 2 + 1 - core
    x_right, x_left, x_far = lax.rem(x + 1, RING), lax.rem(x + RING - 1, RING), lax.rem(x + 2, RING)
    right, left, far = x_right * 2 + core, x_left * 2 + core, x_far * 2 + core
    ys = [lax.rem(y + d, SIDE) for d in range(SIDE)]

    rank = jnp.where(y < SIDE // 2, y, SIDE + SIDE // 2 - 1 - y)

    def signal(semaphore, **where):
        pl.semaphore_signal(semaphore, inc=1, device_id=where, device_id_type=MESH)

    barrier = pltpu.get_barrier_semaphore()
    for peer in (other, right, left):
        signal(barrier, tp=peer)
    for step in range(1, SIDE):
        pl.when(step > z)(functools.partial(signal, barrier, seq=y * SIDE + step))
        pl.when(step > rank)(functools.partial(signal, barrier, seq=Y_ORDER[step] * SIDE + z))
    with jax.named_scope("W_barrier"):
        pl.semaphore_wait(barrier, z + rank + 3)
    for step in range(SIDE - 1):
        pl.when(step < z)(functools.partial(signal, known_z.at[z], seq=y * SIDE + step))
        pl.when(step < rank)(functools.partial(signal, known_y.at[rank], seq=Y_ORDER[step] * SIDE + z))

    def push(src, dst, send, recv, **where):
        copy = pltpu.make_async_remote_copy(
            src_ref=src, dst_ref=dst, send_sem=send, recv_sem=recv, device_id=where, device_id_type=MESH
        )
        copy.start()
        return copy

    def take(src, dst, sem):
        copy = pltpu.make_async_copy(src, dst, sem)
        copy.start()
        return copy

    def await_all(ref, sem):
        pltpu.make_async_copy(ref, ref, sem).wait()

    mover = core == 1
    early, late = z < EARLY, z >= EARLY
    low_z, high_z = pl.ds(0, EARLY), pl.ds(EARLY, EARLY)
    queries = (0, q_hbm, q_mid, q_up, q_all)
    span = (1, kv_hbm, kv_mid, kv_up, kv_all)

    def streams(step, *args):
        step(*queries, *args)
        pl.when(mover)(functools.partial(step, *span, *args))

    def at_z(to):
        return {"seq": y * SIDE + to}

    def at_y(to):
        return {"seq": to * SIDE + z}

    def send_z(i, src, mid, up, every, to):
        push(src.at[:, to], mid.at[z], z_send.at[i], z_recv.at[i, z // EARLY], **at_z(to))

    def send_z_known(to):
        pl.semaphore_wait(known_z.at[to], 1)
        streams(send_z, to)

    def send_up(i, src, mid, up, every, to):
        push(src.at[to, high_z], up.at[y], up_send.at[i], up_recv.at[i], **at_y(to))

    def send_up_known(step):
        pl.semaphore_wait(known_y.at[step], 1)
        streams(send_up, Y_ORDER[step])

    def own_start(i, src, mid, up, every):
        pltpu.make_async_copy(src.at[:, z], mid.at[z], loc_sem.at[2 * i]).start()
        pl.when(early)(pltpu.make_async_copy(src.at[y, high_z], up.at[y], loc_sem.at[2 * i + 1]).start)

    for step in range(SIDE - 1):
        pl.when(step < z)(functools.partial(streams, send_z, step))
    for step in range(SIDE - 1):
        pl.when(jnp.logical_and(early, step < rank))(functools.partial(streams, send_up, Y_ORDER[step]))
    streams(own_start)

    shard = cache_hbm.at[0]
    ring = [
        push(shard, stored.at[t], ring_send.at[0], ring_recv.at[0], tp=right),
        push(shard, stored.at[t], ring_send.at[1], ring_recv.at[1], tp=left),
        push(shard, stored.at[t], ring_send.at[2], ring_recv.at[2], tp=other),
    ]
    own_shard = take(shard, stored.at[t], loc_sem.at[4])
    small = [
        take(plen_hbm, plen, loc_sem.at[5]),
        take(slen_hbm, slen, loc_sem.at[6]),
        take(rs_hbm, rs, loc_sem.at[7]),
    ]
    for load in small:
        load.wait()

    source = rs[pl.ds(z, 1), :].astype(jnp.float32)
    source = jnp.broadcast_to(source, (HD, TOK)).T
    row = lax.broadcasted_iota(jnp.int32, (TOK, HD), 0).astype(jnp.float32)
    lane = lax.broadcasted_iota(jnp.int32, (TOK, HD), 1).astype(jnp.float32)
    places = [
        jnp.sum(jnp.where(source == lane + float(part * HD), row, 0.0), axis=0, keepdims=True)
        for part in range(TOK // HD)
    ]
    place = jnp.concatenate(places, axis=1)
    source = jnp.swapaxes(source.reshape(SIDE, SIDE, ROWS, HD), 0, 1).reshape(TOK, HD)
    for part in range(TOK // HD):
        pick[:, part * HD : (part + 1) * HD] = jnp.where(source == lane + float(part * HD), 1.0, 0.0).astype(
            jnp.bfloat16
        )

    with jax.named_scope("W_upper"):
        for step in range(1, SIDE):
            pl.when(jnp.logical_and(early, step > rank))(functools.partial(send_up_known, step))
        for step in range(1, SIDE):
            open_now = step > z if step < EARLY else jnp.logical_and(late, step > z)
            pl.when(open_now)(functools.partial(send_z_known, step))
        for step in range(1, SIDE):
            pl.when(jnp.logical_and(late, step > rank))(
                functools.partial(pl.semaphore_wait, known_y.at[step], 1)
            )

    low, high = pl.ds(0, SHARD // 2), pl.ds(SHARD // 2, SHARD // 2)
    with jax.named_scope("W_ring01"):
        ring[0].wait_recv()
        ring[1].wait_recv()
    ring.append(push(stored.at[left, low], stored.at[left, low], ring_send.at[3], ring_recv.at[3], tp=right))
    ring.append(push(stored.at[right, high], stored.at[right, high], ring_send.at[4], ring_recv.at[4], tp=left))
    ring.append(push(stored.at[left], stored.at[left], ring_send.at[5], ring_recv.at[5], tp=other))
    ring.append(push(stored.at[right], stored.at[right], ring_send.at[6], ring_recv.at[6], tp=other))

    def send_y(i, src, mid, up, every, part, which, semaphores):
        for d in FAR_FIRST:
            push(mid.at[part, ys[d]], every.at[y, part], y_send.at[i, which], semaphores[i], **at_y(ys[d]))

    def own_wait(i, src, mid, up, every):
        pltpu.make_async_copy(src.at[:, z], mid.at[z], loc_sem.at[2 * i]).wait()

    def low_part(i, src, mid, up, every):
        with jax.named_scope("W_low"):
            own_wait(i, src, mid, up, every)
            await_all(mid.at[pl.ds(0, EARLY - 1)], z_recv.at[i, 0])
        send_y(i, src, mid, up, every, low_z, 0, (q_done, low_done))
        take(mid.at[low_z, y], every.at[y, low_z], loc_sem.at[2 * i])

    def up_wait(i, src, mid, up, every):
        with jax.named_scope("W_up"):
            pltpu.make_async_copy(src.at[y, high_z], up.at[y], loc_sem.at[2 * i + 1]).wait()
            await_all(up.at[pl.ds(0, SIDE - 1)], up_recv.at[i])

    def up_part(i, src, mid, up, every, to):
        push(up.at[:, to - EARLY], every.at[:, z], far_send.at[i], (q_done, low_done)[i], **at_z(to))

    def early_part():
        streams(low_part)
        streams(up_wait)
        for to in range(EARLY, SIDE):
            with jax.named_scope("W_far"):
                pl.semaphore_wait(known_z.at[to], 1)
            streams(up_part, to)

    pl.when(early)(early_part)

    def high_part(i, src, mid, up, every):
        with jax.named_scope("W_high"):
            pl.when(late)(functools.partial(own_wait, i, src, mid, up, every))
            pl.when(late)(functools.partial(await_all, mid.at[pl.ds(0, EARLY - 1)], z_recv.at[i, 1]))
            pl.when(early)(functools.partial(await_all, mid.at[pl.ds(0, EARLY)], z_recv.at[i, 1]))
        send_y(i, src, mid, up, every, high_z, 1, (q_done, high_done.at[y]))
        take(mid.at[high_z, y], every.at[y, high_z], loc_sem.at[2 * i + 1])

    streams(high_part)

    with jax.named_scope("W_ring34"):
        ring[3].wait_recv()
        ring[4].wait_recv()
    ring.append(push(stored.at[far], stored.at[far], ring_send.at[7], ring_recv.at[7], tp=other))

    def own_low_wait(i, src, mid, up, every):
        pltpu.make_async_copy(mid.at[low_z, y], every.at[y, low_z], loc_sem.at[2 * i]).wait()

    def own_high_wait(i, src, mid, up, every):
        pltpu.make_async_copy(mid.at[high_z, y], every.at[y, high_z], loc_sem.at[2 * i + 1]).wait()

    def hand_over():
        with jax.named_scope("W_kvlow"):
            pl.when(early)(functools.partial(own_low_wait, *span))
            pl.when(early)(functools.partial(await_all, kv_all.at[pl.ds(0, SIDE - 1), low_z], low_done))
            pl.when(late)(functools.partial(await_all, kv_all.at[:, low_z], low_done))
        push(kv_all.at[:, low_z], kv_all.at[:, low_z], swap_send, swap_recv, tp=other)
        for step in Y_ORDER:
            piece = kv_all.at[step, high_z]
            with jax.named_scope("W_kv2"):
                pl.when(step == y)(functools.partial(own_high_wait, *span))
                pl.when(step != y)(functools.partial(await_all, piece, high_done.at[step]))
            push(piece, piece, swap_send, swap_recv, tp=other)

    pl.when(mover)(hand_over)

    def early_queries():
        own_low_wait(*queries)
        await_all(q_all.at[pl.ds(0, SIDE - 1)], q_done)

    def late_queries():
        await_all(q_bytes, q_done)

    with jax.named_scope("W_q2"):
        own_high_wait(*queries)
        pl.when(early)(early_queries)
        pl.when(late)(late_queries)
    with jax.named_scope("W_ringall"):
        own_shard.wait()
        for step in (2, 5, 6, 7):
            ring[step].wait_recv()

    rate = math.log2(math.e) / math.sqrt(HD)
    contract = (((1,), (1,)), ((), ()))
    keys = RING * 2 * SHARD
    limit = plen[z]
    live = slen[z]

    def cache_scores(groups):
        rows = slice(groups[0] * GROUP, groups[1] * GROUP)
        rows_q = jnp.dot(pick[rows, :], q_all[...].reshape(TOK, HD), preferred_element_type=jnp.float32)
        rows_q = rows_q.astype(jnp.bfloat16)
        q_tab[rows, :] = rows_q
        scores = lax.dot_general(
            rows_q, stored[:, :, :HD].reshape(keys, HD), contract, preferred_element_type=jnp.float32
        )
        seen = lax.broadcasted_iota(jnp.int32, scores.shape, 1) < limit
        return jnp.where(seen, scores, -jnp.inf)

    def tokens(groups, width):
        count = lax.broadcasted_iota(jnp.int32, ((groups[1] - groups[0]) * GROUP, width), 0)
        in_group = lax.bitwise_and(count, GROUP - 1)
        return (in_group - lax.bitwise_and(in_group, ROWS - 1)) * SIDE + (
            lax.bitwise_and(in_group, ROWS - 1) + ((count - in_group) // SIDE + groups[0] * ROWS)
        )

    def span_scores(groups):
        rows = q_tab[groups[0] * GROUP : groups[1] * GROUP, :]
        scores = lax.dot_general(
            rows, kv_all[:, :, :, :HD].reshape(TOK, HD), contract, preferred_element_type=jnp.float32
        )
        return jnp.where(place <= tokens(groups, TOK).astype(jnp.float32), scores, -jnp.inf)

    def send_out(to, d):
        push(att.at[to, ys[d]], out_ref.at[s], out_send, out_recv, seq=ys[d] * SIDE + to)

    def attend(groups, held, fresh):
        top = jnp.maximum(jnp.max(held, axis=1, keepdims=True), jnp.max(fresh, axis=1, keepdims=True))
        held = jnp.exp2((held - top) * rate).astype(jnp.bfloat16)
        fresh = jnp.exp2((fresh - top) * rate).astype(jnp.bfloat16)
        values = jnp.concatenate([stored[:, :, HD:].reshape(keys, HD), jnp.ones((keys, HD), jnp.bfloat16)], axis=1)
        total = jnp.dot(held, values, preferred_element_type=jnp.float32)
        values = jnp.concatenate([kv_all[:, :, :, HD:].reshape(TOK, HD), jnp.ones((TOK, HD), jnp.bfloat16)], axis=1)
        total = total + jnp.dot(fresh, values, preferred_element_type=jnp.float32)
        result = total[:, :HD] / total[:, HD:]
        result = jnp.where(tokens(groups, HD) < live, result, 0.0).astype(jnp.bfloat16)
        att[groups[0] : groups[1]] = result.reshape(groups[1] - groups[0], SIDE, ROWS, HD)
        for to in range(*groups):
            for d in FAR_FIRST:
                send_out(to, d)
            pl.when(to != z)(functools.partial(send_out, to, 0))

    with jax.named_scope("C_cache0"):
        held = cache_scores(BLOCKS[0])
    with jax.named_scope("W_swap"):
        pl.when(jnp.logical_not(mover))(functools.partial(await_all, kv_all, swap_recv))
    fresh = span_scores(BLOCKS[0])
    for number, groups in enumerate(BLOCKS):
        with jax.named_scope(f"C_block{number}"):
            last = number == len(BLOCKS) - 1
            following = None if last else (cache_scores(BLOCKS[number + 1]), span_scores(BLOCKS[number + 1]))
            attend(groups, held, fresh)
            if not last:
                held, fresh = following
    own = take(att.at[z, y], out_ref.at[s], loc_sem.at[0])

    for step in range(8):
        ring[step].wait_send()
    def all_sent(i, src, mid, up, every):
        def early_sent():
            await_all(mid.at[pl.ds(0, EARLY - 1)], z_send.at[i])
            await_all(up.at[pl.ds(0, SIDE - 1)], up_send.at[i])
            await_all(up.at[pl.ds(0, SIDE - 1)], y_send.at[i, 0])
            await_all(mid.at[pl.ds(0, EARLY)], far_send.at[i])

        pl.when(early)(early_sent)
        pl.when(late)(functools.partial(await_all, mid.at[pl.ds(0, SIDE - 1)], z_send.at[i]))
        await_all(up.at[pl.ds(0, SIDE - 1)], y_send.at[i, 1])

    streams(all_sent)
    pl.when(mover)(functools.partial(await_all, kv_all, swap_send))
    own.wait()
    peers = pl.ds(0, SIDE * SIDE - 1)
    with jax.named_scope("W_outsend"):
        await_all(out_ref.at[peers], out_send)
    with jax.named_scope("W_out"):
        await_all(out_ref.at[peers], out_recv)


def on_device(queries, span_kv, cache, prefix_len, span_len, row_source):
    shape = queries.shape
    hbm = pl.BlockSpec(memory_space=pl.ANY)
    tile = (SIDE, SIDE, ROWS, HD)
    out = pl.pallas_call(
        kernel,
        out_shape=pltpu.VMEM((SIDE * SIDE, ROWS, HD), jnp.bfloat16),
        in_specs=[hbm] * 6,
        out_specs=pl.BlockSpec(memory_space=pltpu.VMEM),
        scratch_shapes=[
            pltpu.VMEM(tile, jnp.bfloat16),
            pltpu.VMEM((SIDE, EARLY, ROWS, HD), jnp.bfloat16),
            pltpu.VMEM(tile, jnp.bfloat16),
            pltpu.VMEM((SIDE, SIDE, ROWS, 2 * HD), jnp.bfloat16),
            pltpu.VMEM((SIDE, EARLY, ROWS, 2 * HD), jnp.bfloat16),
            pltpu.VMEM((SIDE, SIDE, ROWS, 2 * HD), jnp.bfloat16),
            pltpu.VMEM((RING * 2, SHARD, 2 * HD), jnp.bfloat16),
            pltpu.SMEM((8,), jnp.int32),
            pltpu.SMEM((8,), jnp.int32),
            pltpu.VMEM((8, TOK), jnp.int32),
            pltpu.VMEM((TOK, TOK), jnp.bfloat16),
            pltpu.VMEM((TOK, HD), jnp.bfloat16),
            pltpu.VMEM(tile, jnp.bfloat16),
            pltpu.SemaphoreType.REGULAR((SIDE,)),
            pltpu.SemaphoreType.REGULAR((SIDE,)),
            pltpu.VMEM((15, EARLY, ROWS, HD), jnp.bfloat16),
            pltpu.SemaphoreType.DMA((8,)),
            pltpu.SemaphoreType.DMA((2,)),
            pltpu.SemaphoreType.DMA((2, 2)),
            pltpu.SemaphoreType.DMA((2,)),
            pltpu.SemaphoreType.DMA((2,)),
            pltpu.SemaphoreType.DMA((2, 2)),
            pltpu.SemaphoreType.DMA((2,)),
            pltpu.SemaphoreType.DMA,
            pltpu.SemaphoreType.DMA,
            pltpu.SemaphoreType.DMA((SIDE,)),
            pltpu.SemaphoreType.DMA,
            pltpu.SemaphoreType.DMA,
            pltpu.SemaphoreType.DMA,
            pltpu.SemaphoreType.DMA,
            pltpu.SemaphoreType.DMA((8,)),
            pltpu.SemaphoreType.DMA((8,)),
        ],
        compiler_params=pltpu.CompilerParams(collective_id=0, has_side_effects=True),
    )(
        queries.reshape(tile),
        span_kv,
        cache,
        prefix_len,
        span_len,
        row_source,
    )
    return out.reshape(shape)


def solution(mesh):
    in_specs = (
        P(None, None, "seq", "tp", None),
        P(None, None, "seq", None),
        P("seq", "tp", None),
        P(),
        P(),
        P(),
    )
    out_specs = P(None, None, "seq", "tp", None)
    return jax.shard_map(on_device, mesh=mesh, in_specs=in_specs, out_specs=out_specs, check_vma=False)
```

time: 35 us -> 35.1 us (level)
  the two profiles are of different devices: /device:TPU:8 before, /device:TPU:6 now
where the time goes in v5:
time: 35.1 us; the launch traced here: 34.9 us
  Pallas kernels  34.3 us (98%)
  local copies, waits for them, and re-layouts  0.66 us (2%)
    pallas_call x1, Pallas kernels, on_device(): pl.pallas_call(kernel, out_shape=pltpu.VMEM((SIDE * SIDE, ROWS, HD), jnp....  34.3 us

profile of v5, /device:TPU:6, one launch (start us, length us, event | category | flops | bytes accessed | tf_op | source)
XLA Modules:
  0.0 34.9 jit_solution(12733097833026266701)
XLA Ops:
  0.0 34.3 %shard_map.64 = bf16[64,8,128]{2,1,0:T(8,128)(2,1)S(1)} custom-call(bf16[8,8,8,128]{3,2,1,0:T(8,128)(2,1)} %bitcast.5, bf16[8,8,8,256]{3,2,1,0:T(8,128)(2,1)} %kv_hbm.1, bf16[1,256,256]{2,1,0:T(8,128)(2,1)} %cache_hbm.1, s32[8]{0:T(128)} %plen_hbm.1, s32[8]{0:T(128)} %slen_hbm.1, s32[8,512]{1,0:T(8,128)} %rs_hbm.1), custom_call_target="tpu_custom_call" | custom-call | tf_op jit(solution)/shard_map/pallas_call | solution.py:372
  34.3 0.7 %copy.9 = bf16[8,8,8,1,128]{4,2,3,1,0:T(8,128)(2,1)} copy(bf16[8,8,8,1,128]{4,2,3,1,0:T(8,128)(2,1)S(1)} %bitcast.4) | data formatting | bytes 262144

commit v6 on v5

--- a/solution.py
+++ b/solution.py
@@ -111,8 +111,8 @@
     span = (1, kv_hbm, kv_mid, kv_up, kv_all)
 
     def streams(step, *args):
+        pl.when(mover)(functools.partial(step, *span, *args))
         step(*queries, *args)
-        pl.when(mover)(functools.partial(step, *span, *args))
 
     def at_z(to):
         return {"seq": y * SIDE + to}
@@ -138,7 +138,7 @@
         pltpu.make_async_copy(src.at[:, z], mid.at[z], loc_sem.at[2 * i]).start()
         pl.when(early)(pltpu.make_async_copy(src.at[y, high_z], up.at[y], loc_sem.at[2 * i + 1]).start)
 
-    for step in range(SIDE - 1):
+    for step in reversed(range(SIDE - 1)):
         pl.when(step < z)(functools.partial(streams, send_z, step))
     for step in range(SIDE - 1):
         pl.when(jnp.logical_and(early, step < rank))(functools.partial(streams, send_up, Y_ORDER[step]))
@@ -205,7 +205,7 @@
         with jax.named_scope("W_low"):
             own_wait(i, src, mid, up, every)
             await_all(mid.at[pl.ds(0, EARLY - 1)], z_recv.at[i, 0])
-        send_y(i, src, mid, up, every, low_z, 0, (q_done, low_done))
+        send_y(i, src, mid, up, every, low_z, 0, (q_done, low_done.at[y]))
         take(mid.at[low_z, y], every.at[y, low_z], loc_sem.at[2 * i])
 
     def up_wait(i, src, mid, up, every):
@@ -214,7 +214,7 @@
             await_all(up.at[pl.ds(0, SIDE - 1)], up_recv.at[i])
 
     def up_part(i, src, mid, up, every, to):
-        push(up.at[:, to - EARLY], every.at[:, z], far_send.at[i], (q_done, low_done)[i], **at_z(to))
+        push(up.at[:, to - EARLY], every.at[:, z], far_send.at[i], (q_done, low_done.at[z])[i], **at_z(to))
 
     def early_part():
         streams(low_part)
@@ -247,18 +247,48 @@
     def own_high_wait(i, src, mid, up, every):
         pltpu.make_async_copy(mid.at[high_z, y], every.at[y, high_z], loc_sem.at[2 * i + 1]).wait()
 
+    def hand(piece):
+        push(piece, piece, swap_send, swap_recv, tp=other)
+
+    def hand_low_y(step):
+        piece = kv_all.at[step, low_z]
+        with jax.named_scope("W_kvlow"):
+            pl.when(step == y)(functools.partial(own_low_wait, *span))
+            pl.when(step != y)(functools.partial(await_all, piece, low_done.at[step]))
+        hand(piece)
+
+    def hand_low_z(step):
+        piece = kv_all.at[:, step]
+        with jax.named_scope("W_kvlow"):
+            await_all(piece, low_done.at[step])
+        hand(piece)
+
+    def hand_high(step):
+        piece = kv_all.at[step, high_z]
+        with jax.named_scope("W_kv2"):
+            pl.when(step == y)(functools.partial(own_high_wait, *span))
+            pl.when(step != y)(functools.partial(await_all, piece, high_done.at[step]))
+        hand(piece)
+
+    def hand_over_early():
+        for step in Y_ORDER:
+            hand_low_y(step)
+        for step in Y_ORDER:
+            hand_high(step)
+
+    def hand_over_late():
+        hand_low_z(0)
+        for step in Y_ORDER[:4]:
+            hand_high(step)
+        hand_low_z(1)
+        for step in Y_ORDER[4:]:
+            hand_high(step)
+        hand_low_z(2)
+        hand_low_z(3)
+
     def hand_over():
-        with jax.named_scope("W_kvlow"):
-            pl.when(early)(functools.partial(own_low_wait, *span))
-            pl.when(early)(functools.partial(await_all, kv_all.at[pl.ds(0, SIDE - 1), low_z], low_done))
-            pl.when(late)(functools.partial(await_all, kv_all.at[:, low_z], low_done))
-        push(kv_all.at[:, low_z], kv_all.at[:, low_z], swap_send, swap_recv, tp=other)
-        for step in Y_ORDER:
-            piece = kv_all.at[step, high_z]
-            with jax.named_scope("W_kv2"):
-                pl.when(step == y)(functools.partial(own_high_wait, *span))
-                pl.when(step != y)(functools.partial(await_all, piece, high_done.at[step]))
-            push(piece, piece, swap_send, swap_recv, tp=other)
+        pl.when(early)(hand_over_early)
+        pl.when(late)(hand_over_late)
 
     pl.when(mover)(hand_over)
 
@@ -399,7 +429,7 @@
             pltpu.SemaphoreType.DMA((2, 2)),
             pltpu.SemaphoreType.DMA((2,)),
             pltpu.SemaphoreType.DMA,
-            pltpu.SemaphoreType.DMA,
+            pltpu.SemaphoreType.DMA((SIDE,)),
             pltpu.SemaphoreType.DMA((SIDE,)),
             pltpu.SemaphoreType.DMA,
             pltpu.SemaphoreType.DMA,

time: 35.1 us -> 34.7 us (0.989)
  the two profiles are of different devices: /device:TPU:6 before, /device:TPU:1 now
where the time goes in v6:
time: 34.7 us; the launch traced here: 34.3 us
  Pallas kernels  33.6 us (97%)
  local copies, waits for them, and re-layouts  0.66 us (2%)
    pallas_call x1, Pallas kernels, on_device(): pl.pallas_call(kernel, out_shape=pltpu.VMEM((SIDE * SIDE, ROWS, HD), jnp....  33.6 us

profile of v6, /device:TPU:1, one launch (start us, length us, event | category | flops | bytes accessed | tf_op | source)
XLA Modules:
  0.0 34.3 jit_solution(2981476922255395832)
XLA Ops:
  0.0 33.6 %shard_map.64 = bf16[64,8,128]{2,1,0:T(8,128)(2,1)S(1)} custom-call(bf16[8,8,8,128]{3,2,1,0:T(8,128)(2,1)} %bitcast.5, bf16[8,8,8,256]{3,2,1,0:T(8,128)(2,1)} %kv_hbm.1, bf16[1,256,256]{2,1,0:T(8,128)(2,1)} %cache_hbm.1, s32[8]{0:T(128)} %plen_hbm.1, s32[8]{0:T(128)} %slen_hbm.1, s32[8,512]{1,0:T(8,128)} %rs_hbm.1), custom_call_target="tpu_custom_call" | custom-call | tf_op jit(solution)/shard_map/pallas_call | solution.py:402
  33.6 0.7 %copy.9 = bf16[8,8,8,1,128]{4,2,3,1,0:T(8,128)(2,1)} copy(bf16[8,8,8,1,128]{4,2,3,1,0:T(8,128)(2,1)S(1)} %bitcast.4) | data formatting | bytes 262144

commit v7 on v6

--- a/solution.py
+++ b/solution.py
@@ -16,6 +16,9 @@
 TOK = 512
 SHARD = 256
 EARLY = 4
+EARLY_TILES = 3 * 8 + 3 * 7 * 4 + 4 * 8
+LATE_TILES = 7 * 8 + 7 * 4
+OTHER_TILES = 7 * 64 + 63
 GROUP = 64
 FAR_FIRST = (4, 3, 5, 2, 6, 1, 7)
 BLOCKS = ((0, 2), (2, 4), (4, 6), (6, 8))
@@ -45,22 +48,17 @@
     att,
     known_y,
     known_z,
-    q_bytes,
+    nothing,
     loc_sem,
-    z_send,
+    sent,
+    moved,
     z_recv,
-    up_send,
     up_recv,
-    y_send,
-    far_send,
     q_done,
     low_done,
     high_done,
-    swap_send,
     swap_recv,
-    out_send,
     out_recv,
-    ring_send,
     ring_recv,
 ):
     s = lax.axis_index("seq")
@@ -121,14 +119,14 @@
         return {"seq": to * SIDE + z}
 
     def send_z(i, src, mid, up, every, to):
-        push(src.at[:, to], mid.at[z], z_send.at[i], z_recv.at[i, z // EARLY], **at_z(to))
+        push(src.at[:, to], mid.at[z], moved, z_recv.at[i, z // EARLY], **at_z(to))
 
     def send_z_known(to):
         pl.semaphore_wait(known_z.at[to], 1)
         streams(send_z, to)
 
     def send_up(i, src, mid, up, every, to):
-        push(src.at[to, high_z], up.at[y], up_send.at[i], up_recv.at[i], **at_y(to))
+        push(src.at[to, high_z], up.at[y], moved, up_recv.at[i], **at_y(to))
 
     def send_up_known(step):
         pl.semaphore_wait(known_y.at[step], 1)
@@ -145,11 +143,9 @@
     streams(own_start)
 
     shard = cache_hbm.at[0]
-    ring = [
-        push(shard, stored.at[t], ring_send.at[0], ring_recv.at[0], tp=right),
-        push(shard, stored.at[t], ring_send.at[1], ring_recv.at[1], tp=left),
-        push(shard, stored.at[t], ring_send.at[2], ring_recv.at[2], tp=other),
-    ]
+    push(shard, stored.at[t], sent, ring_recv.at[0], tp=right)
+    push(shard, stored.at[t], sent, ring_recv.at[0], tp=left)
+    push(shard, stored.at[t], sent, ring_recv.at[2], tp=other)
     own_shard = take(shard, stored.at[t], loc_sem.at[4])
     small = [
         take(plen_hbm, plen, loc_sem.at[5]),
@@ -187,16 +183,15 @@
 
     low, high = pl.ds(0, SHARD // 2), pl.ds(SHARD // 2, SHARD // 2)
     with jax.named_scope("W_ring01"):
-        ring[0].wait_recv()
-        ring[1].wait_recv()
-    ring.append(push(stored.at[left, low], stored.at[left, low], ring_send.at[3], ring_recv.at[3], tp=right))
-    ring.append(push(stored.at[right, high], stored.at[right, high], ring_send.at[4], ring_recv.at[4], tp=left))
-    ring.append(push(stored.at[left], stored.at[left], ring_send.at[5], ring_recv.at[5], tp=other))
-    ring.append(push(stored.at[right], stored.at[right], ring_send.at[6], ring_recv.at[6], tp=other))
+        await_all(stored.at[pl.ds(0, 2)], ring_recv.at[0])
+    push(stored.at[left, low], stored.at[left, low], sent, ring_recv.at[1], tp=right)
+    push(stored.at[right, high], stored.at[right, high], sent, ring_recv.at[1], tp=left)
+    push(stored.at[left], stored.at[left], sent, ring_recv.at[2], tp=other)
+    push(stored.at[right], stored.at[right], sent, ring_recv.at[2], tp=other)
 
     def send_y(i, src, mid, up, every, part, which, semaphores):
         for d in FAR_FIRST:
-            push(mid.at[part, ys[d]], every.at[y, part], y_send.at[i, which], semaphores[i], **at_y(ys[d]))
+            push(mid.at[part, ys[d]], every.at[y, part], moved, semaphores[i], **at_y(ys[d]))
 
     def own_wait(i, src, mid, up, every):
         pltpu.make_async_copy(src.at[:, z], mid.at[z], loc_sem.at[2 * i]).wait()
@@ -205,7 +200,7 @@
         with jax.named_scope("W_low"):
             own_wait(i, src, mid, up, every)
             await_all(mid.at[pl.ds(0, EARLY - 1)], z_recv.at[i, 0])
-        send_y(i, src, mid, up, every, low_z, 0, (q_done, low_done.at[y]))
+        send_y(i, src, mid, up, every, low_z, 0, (q_done, low_done.at[0]))
         take(mid.at[low_z, y], every.at[y, low_z], loc_sem.at[2 * i])
 
     def up_wait(i, src, mid, up, every):
@@ -214,7 +209,7 @@
             await_all(up.at[pl.ds(0, SIDE - 1)], up_recv.at[i])
 
     def up_part(i, src, mid, up, every, to):
-        push(up.at[:, to - EARLY], every.at[:, z], far_send.at[i], (q_done, low_done.at[z])[i], **at_z(to))
+        push(up.at[:, to - EARLY], every.at[:, z], moved, (q_done, low_done.at[z])[i], **at_z(to))
 
     def early_part():
         streams(low_part)
@@ -237,9 +232,8 @@
     streams(high_part)
 
     with jax.named_scope("W_ring34"):
-        ring[3].wait_recv()
-        ring[4].wait_recv()
-    ring.append(push(stored.at[far], stored.at[far], ring_send.at[7], ring_recv.at[7], tp=other))
+        await_all(stored.at[0], ring_recv.at[1])
+    push(stored.at[far], stored.at[far], sent, ring_recv.at[2], tp=other)
 
     def own_low_wait(i, src, mid, up, every):
         pltpu.make_async_copy(mid.at[low_z, y], every.at[y, low_z], loc_sem.at[2 * i]).wait()
@@ -248,14 +242,13 @@
         pltpu.make_async_copy(mid.at[high_z, y], every.at[y, high_z], loc_sem.at[2 * i + 1]).wait()
 
     def hand(piece):
-        push(piece, piece, swap_send, swap_recv, tp=other)
-
-    def hand_low_y(step):
-        piece = kv_all.at[step, low_z]
+        push(piece, piece, moved, swap_recv, tp=other)
+
+    def hand_low_all():
         with jax.named_scope("W_kvlow"):
-            pl.when(step == y)(functools.partial(own_low_wait, *span))
-            pl.when(step != y)(functools.partial(await_all, piece, low_done.at[step]))
-        hand(piece)
+            own_low_wait(*span)
+            await_all(kv_all.at[pl.ds(0, SIDE - 1), low_z], low_done.at[0])
+        hand(kv_all.at[:, low_z])
 
     def hand_low_z(step):
         piece = kv_all.at[:, step]
@@ -271,8 +264,7 @@
         hand(piece)
 
     def hand_over_early():
-        for step in Y_ORDER:
-            hand_low_y(step)
+        hand_low_all()
         for step in Y_ORDER:
             hand_high(step)
 
@@ -297,7 +289,7 @@
         await_all(q_all.at[pl.ds(0, SIDE - 1)], q_done)
 
     def late_queries():
-        await_all(q_bytes, q_done)
+        await_all(nothing.at[pl.ds(0, (SIDE - 1) * EARLY + SIDE * EARLY)], q_done)
 
     with jax.named_scope("W_q2"):
         own_high_wait(*queries)
@@ -305,8 +297,7 @@
         pl.when(late)(late_queries)
     with jax.named_scope("W_ringall"):
         own_shard.wait()
-        for step in (2, 5, 6, 7):
-            ring[step].wait_recv()
+        await_all(stored.at[pl.ds(0, RING)], ring_recv.at[2])
 
     rate = math.log2(math.e) / math.sqrt(HD)
     contract = (((1,), (1,)), ((), ()))
@@ -340,16 +331,30 @@
         return jnp.where(place <= tokens(groups, TOK).astype(jnp.float32), scores, -jnp.inf)
 
     def send_out(to, d):
-        push(att.at[to, ys[d]], out_ref.at[s], out_send, out_recv, seq=ys[d] * SIDE + to)
-
-    def attend(groups, held, fresh):
+        push(att.at[to, ys[d]], out_ref.at[s], sent, out_recv, seq=ys[d] * SIDE + to)
+
+    def cache_part(held):
+        top = jnp.max(held, axis=1, keepdims=True)
+        held = jnp.exp2((held - top) * rate).astype(jnp.bfloat16)
+        values = jnp.concatenate([stored[:, :, HD:].reshape(keys, HD), jnp.ones((keys, HD), jnp.bfloat16)], axis=1)
+        return top, jnp.dot(held, values, preferred_element_type=jnp.float32)
+
+    def span_part(fresh, top):
+        fresh = jnp.exp2((fresh - top) * rate).astype(jnp.bfloat16)
+        values = jnp.concatenate([kv_all[:, :, :, HD:].reshape(TOK, HD), jnp.ones((TOK, HD), jnp.bfloat16)], axis=1)
+        return jnp.dot(fresh, values, preferred_element_type=jnp.float32)
+
+    def attend(held, fresh):
         top = jnp.maximum(jnp.max(held, axis=1, keepdims=True), jnp.max(fresh, axis=1, keepdims=True))
         held = jnp.exp2((held - top) * rate).astype(jnp.bfloat16)
-        fresh = jnp.exp2((fresh - top) * rate).astype(jnp.bfloat16)
         values = jnp.concatenate([stored[:, :, HD:].reshape(keys, HD), jnp.ones((keys, HD), jnp.bfloat16)], axis=1)
-        total = jnp.dot(held, values, preferred_element_type=jnp.float32)
-        values = jnp.concatenate([kv_all[:, :, :, HD:].reshape(TOK, HD), jnp.ones((TOK, HD), jnp.bfloat16)], axis=1)
-        total = total + jnp.dot(fresh, values, preferred_element_type=jnp.float32)
+        return jnp.dot(held, values, preferred_element_type=jnp.float32) + span_part(fresh, top)
+
+    def attend_late(before, total, fresh):
+        top = jnp.maximum(before, jnp.max(fresh, axis=1, keepdims=True))
+        return total * jnp.exp2((before - top) * rate) + span_part(fresh, top)
+
+    def finish(groups, total):
         result = total[:, :HD] / total[:, HD:]
         result = jnp.where(tokens(groups, HD) < live, result, 0.0).astype(jnp.bfloat16)
         att[groups[0] : groups[1]] = result.reshape(groups[1] - groups[0], SIDE, ROWS, HD)
@@ -359,38 +364,33 @@
             pl.when(to != z)(functools.partial(send_out, to, 0))
 
     with jax.named_scope("C_cache0"):
-        held = cache_scores(BLOCKS[0])
+        top, total = cache_part(cache_scores(BLOCKS[0]))
+        held = [None] + [cache_scores(groups) for groups in BLOCKS[1:1]]
     with jax.named_scope("W_swap"):
         pl.when(jnp.logical_not(mover))(functools.partial(await_all, kv_all, swap_recv))
     fresh = span_scores(BLOCKS[0])
     for number, groups in enumerate(BLOCKS):
         with jax.named_scope(f"C_block{number}"):
-            last = number == len(BLOCKS) - 1
-            following = None if last else (cache_scores(BLOCKS[number + 1]), span_scores(BLOCKS[number + 1]))
-            attend(groups, held, fresh)
-            if not last:
-                held, fresh = following
+            if number + 1 < len(BLOCKS):
+                if number + 1 >= len(held):
+                    held.append(cache_scores(BLOCKS[number + 1]))
+                following = span_scores(BLOCKS[number + 1])
+            if number == 0:
+                total = attend_late(top, total, fresh)
+            else:
+                total = attend(held[number], fresh)
+            finish(groups, total)
+            fresh = following
     own = take(att.at[z, y], out_ref.at[s], loc_sem.at[0])
 
-    for step in range(8):
-        ring[step].wait_send()
-    def all_sent(i, src, mid, up, every):
-        def early_sent():
-            await_all(mid.at[pl.ds(0, EARLY - 1)], z_send.at[i])
-            await_all(up.at[pl.ds(0, SIDE - 1)], up_send.at[i])
-            await_all(up.at[pl.ds(0, SIDE - 1)], y_send.at[i, 0])
-            await_all(mid.at[pl.ds(0, EARLY)], far_send.at[i])
-
-        pl.when(early)(early_sent)
-        pl.when(late)(functools.partial(await_all, mid.at[pl.ds(0, SIDE - 1)], z_send.at[i]))
-        await_all(up.at[pl.ds(0, SIDE - 1)], y_send.at[i, 1])
-
-    streams(all_sent)
-    pl.when(mover)(functools.partial(await_all, kv_all, swap_send))
+    await_all(nothing.at[pl.ds(0, OTHER_TILES)], sent)
+    for rows, count in ((early, EARLY_TILES), (late, LATE_TILES)):
+        mine = jnp.logical_and(rows, mover)
+        pl.when(mine)(functools.partial(await_all, nothing.at[pl.ds(0, 3 * count + 128)], moved))
+        mine = jnp.logical_and(rows, jnp.logical_not(mover))
+        pl.when(mine)(functools.partial(await_all, nothing.at[pl.ds(0, count)], moved))
     own.wait()
     peers = pl.ds(0, SIDE * SIDE - 1)
-    with jax.named_scope("W_outsend"):
-        await_all(out_ref.at[peers], out_send)
     with jax.named_scope("W_out"):
         await_all(out_ref.at[peers], out_recv)
 
@@ -420,23 +420,18 @@
             pltpu.VMEM(tile, jnp.bfloat16),
             pltpu.SemaphoreType.REGULAR((SIDE,)),
             pltpu.SemaphoreType.REGULAR((SIDE,)),
-            pltpu.VMEM((15, EARLY, ROWS, HD), jnp.bfloat16),
+            pltpu.VMEM((3 * EARLY_TILES + 128, ROWS, HD), jnp.bfloat16),
             pltpu.SemaphoreType.DMA((8,)),
-            pltpu.SemaphoreType.DMA((2,)),
-            pltpu.SemaphoreType.DMA((2, 2)),
-            pltpu.SemaphoreType.DMA((2,)),
-            pltpu.SemaphoreType.DMA((2,)),
+            pltpu.SemaphoreType.DMA,
+            pltpu.SemaphoreType.DMA,
             pltpu.SemaphoreType.DMA((2, 2)),
             pltpu.SemaphoreType.DMA((2,)),
             pltpu.SemaphoreType.DMA,
-            pltpu.SemaphoreType.DMA((SIDE,)),
+            pltpu.SemaphoreType.DMA((EARLY,)),
             pltpu.SemaphoreType.DMA((SIDE,)),
             pltpu.SemaphoreType.DMA,
             pltpu.SemaphoreType.DMA,
-            pltpu.SemaphoreType.DMA,
-            pltpu.SemaphoreType.DMA,
-            pltpu.SemaphoreType.DMA((8,)),
-            pltpu.SemaphoreType.DMA((8,)),
+            pltpu.SemaphoreType.DMA((3,)),
         ],
         compiler_params=pltpu.CompilerParams(collective_id=0, has_side_effects=True),
     )(

time: 34.7 us -> 34.3 us (0.988)
  no operation moved by 1% of the time
where the time goes in v7:
time: 34.3 us; the launch traced here: 34.2 us
  Pallas kernels  33.5 us (98%)
  local copies, waits for them, and re-layouts  0.66 us (2%)
    pallas_call x1, Pallas kernels, on_device(): pl.pallas_call(kernel, out_shape=pltpu.VMEM((SIDE * SIDE, ROWS, HD), jnp....  33.5 us

profile of v7, /device:TPU:1, one launch (start us, length us, event | category | flops | bytes accessed | tf_op | source)
XLA Modules:
  0.0 34.2 jit_solution(6684892544519814831)
XLA Ops:
  0.0 33.5 %shard_map.64 = bf16[64,8,128]{2,1,0:T(8,128)(2,1)S(1)} custom-call(bf16[8,8,8,128]{3,2,1,0:T(8,128)(2,1)} %bitcast.5, bf16[8,8,8,256]{3,2,1,0:T(8,128)(2,1)} %kv_hbm.1, bf16[1,256,256]{2,1,0:T(8,128)(2,1)} %cache_hbm.1, s32[8]{0:T(128)} %plen_hbm.1, s32[8]{0:T(128)} %slen_hbm.1, s32[8,512]{1,0:T(8,128)} %rs_hbm.1), custom_call_target="tpu_custom_call" | custom-call | tf_op jit(solution)/shard_map/pallas_call | solution.py:402
  33.5 0.7 %copy.9 = bf16[8,8,8,1,128]{4,2,3,1,0:T(8,128)(2,1)} copy(bf16[8,8,8,1,128]{4,2,3,1,0:T(8,128)(2,1)S(1)} %bitcast.4) | data formatting | bytes 262144

commit v8 on v7

--- a/solution.py
+++ b/solution.py
@@ -217,7 +217,9 @@
         for to in range(EARLY, SIDE):
             with jax.named_scope("W_far"):
                 pl.semaphore_wait(known_z.at[to], 1)
-            streams(up_part, to)
+            pl.when(mover)(functools.partial(up_part, *span, to))
+        for to in range(EARLY, SIDE):
+            up_part(*queries, to)
 
     pl.when(early)(early_part)
 
@@ -365,21 +367,19 @@
 
     with jax.named_scope("C_cache0"):
         top, total = cache_part(cache_scores(BLOCKS[0]))
-        held = [None] + [cache_scores(groups) for groups in BLOCKS[1:1]]
+        held = [None, cache_scores(BLOCKS[1])]
     with jax.named_scope("W_swap"):
         pl.when(jnp.logical_not(mover))(functools.partial(await_all, kv_all, swap_recv))
-    fresh = span_scores(BLOCKS[0])
-    for number, groups in enumerate(BLOCKS):
+    with jax.named_scope("C_block0"):
+        finish(BLOCKS[0], attend_late(top, total, span_scores(BLOCKS[0])))
+    fresh = span_scores(BLOCKS[1])
+    for number in range(1, len(BLOCKS)):
         with jax.named_scope(f"C_block{number}"):
+            following = None
             if number + 1 < len(BLOCKS):
-                if number + 1 >= len(held):
-                    held.append(cache_scores(BLOCKS[number + 1]))
+                held.append(cache_scores(BLOCKS[number + 1]))
                 following = span_scores(BLOCKS[number + 1])
-            if number == 0:
-                total = attend_late(top, total, fresh)
-            else:
-                total = attend(held[number], fresh)
-            finish(groups, total)
+            finish(BLOCKS[number], attend(held[number], fresh))
             fresh = following
     own = take(att.at[z, y], out_ref.at[s], loc_sem.at[0])
 

time: 34.3 us -> 34 us (level)
  Pallas kernels: 33.5 us -> 32.9 us
    pallas_call x1, Pallas kernels: 33.5 us -> 32.9 us  [on_device(): pl.pallas_call(kernel, out_shape=pltpu.VMEM((SIDE * SIDE, ROWS, HD), jnp....]
where the time goes in v8:
time: 34 us; the launch traced here: 33.6 us
  Pallas kernels  32.9 us (97%)
  local copies, waits for them, and re-layouts  0.66 us (2%)
    pallas_call x1, Pallas kernels, on_device(): pl.pallas_call(kernel, out_shape=pltpu.VMEM((SIDE * SIDE, ROWS, HD), jnp....  32.9 us

profile of v8, /device:TPU:1, one launch (start us, length us, event | category | flops | bytes accessed | tf_op | source)
XLA Modules:
  0.0 33.6 jit_solution(887802704430760520)
XLA Ops:
  0.0 32.9 %shard_map.64 = bf16[64,8,128]{2,1,0:T(8,128)(2,1)S(1)} custom-call(bf16[8,8,8,128]{3,2,1,0:T(8,128)(2,1)} %bitcast.5, bf16[8,8,8,256]{3,2,1,0:T(8,128)(2,1)} %kv_hbm.1, bf16[1,256,256]{2,1,0:T(8,128)(2,1)} %cache_hbm.1, s32[8]{0:T(128)} %plen_hbm.1, s32[8]{0:T(128)} %slen_hbm.1, s32[8,512]{1,0:T(8,128)} %rs_hbm.1), custom_call_target="tpu_custom_call" | custom-call | tf_op jit(solution)/shard_map/pallas_call | solution.py:402
  32.9 0.7 %copy.9 = bf16[8,8,8,1,128]{4,2,3,1,0:T(8,128)(2,1)} copy(bf16[8,8,8,1,128]{4,2,3,1,0:T(8,128)(2,1)S(1)} %bitcast.4) | data formatting | bytes 262144

commit v9 on v8

--- a/solution.py
+++ b/solution.py
@@ -22,7 +22,7 @@
 GROUP = 64
 FAR_FIRST = (4, 3, 5, 2, 6, 1, 7)
 BLOCKS = ((0, 2), (2, 4), (4, 6), (6, 8))
-Y_ORDER = (0, 1, 2, 3, 7, 6, 5, 4)
+Y_ORDER = (0, 1, 2, 3, 4, 5, 6, 7)
 
 
 def kernel(
@@ -70,7 +70,7 @@
     right, left, far = x_right * 2 + core, x_left * 2 + core, x_far * 2 + core
     ys = [lax.rem(y + d, SIDE) for d in range(SIDE)]
 
-    rank = jnp.where(y < SIDE // 2, y, SIDE + SIDE // 2 - 1 - y)
+    rank = y
 
     def signal(semaphore, **where):
         pl.semaphore_signal(semaphore, inc=1, device_id=where, device_id_type=MESH)

time: 34 us -> 34.5 us (1.015)
  Pallas kernels: 32.9 us -> 33.7 us
    pallas_call x1, Pallas kernels: 32.9 us -> 33.7 us  [on_device(): pl.pallas_call(kernel, out_shape=pltpu.VMEM((SIDE * SIDE, ROWS, HD), jnp....]
where the time goes in v9:
time: 34.5 us; the launch traced here: 34.4 us
  Pallas kernels  33.7 us (98%)
  local copies, waits for them, and re-layouts  0.66 us (2%)
    pallas_call x1, Pallas kernels, on_device(): pl.pallas_call(kernel, out_shape=pltpu.VMEM((SIDE * SIDE, ROWS, HD), jnp....  33.7 us

profile of v9, /device:TPU:1, one launch (start us, length us, event | category | flops | bytes accessed | tf_op | source)
XLA Modules:
  0.0 34.4 jit_solution(8808912826301447962)
XLA Ops:
  0.0 33.7 %shard_map.64 = bf16[64,8,128]{2,1,0:T(8,128)(2,1)S(1)} custom-call(bf16[8,8,8,128]{3,2,1,0:T(8,128)(2,1)} %bitcast.5, bf16[8,8,8,256]{3,2,1,0:T(8,128)(2,1)} %kv_hbm.1, bf16[1,256,256]{2,1,0:T(8,128)(2,1)} %cache_hbm.1, s32[8]{0:T(128)} %plen_hbm.1, s32[8]{0:T(128)} %slen_hbm.1, s32[8,512]{1,0:T(8,128)} %rs_hbm.1), custom_call_target="tpu_custom_call" | custom-call | tf_op jit(solution)/shard_map/pallas_call | solution.py:402
  33.8 0.7 %copy.9 = bf16[8,8,8,1,128]{4,2,3,1,0:T(8,128)(2,1)} copy(bf16[8,8,8,1,128]{4,2,3,1,0:T(8,128)(2,1)S(1)} %bitcast.4) | data formatting | bytes 262144
